TPU v7x, 128 devices: a whole 4x4x4 slice. The times are simulated.
128 devices in a mesh: dp: 32 (over z, x, core), mp: 4 (over y).
Axes of the slice: x: 4, y: 4, z: 4, core: 2. Of those that a mesh axis runs over, the one named last changes fastest.
Arguments:
- feat_values: bfloat16 [262144, 8, 128], P('dp', 'mp'), may hold values from -6 to 6
- feat_blocks: int32 [262144, 8], P('dp', 'mp'), may hold values from 0 to 127
- fixed_coef: float32 [128, 128], replicated, may hold values from -0.1875 to 0.1875
- member_of: int32 [262144, 1], P(('dp', 'mp')), may hold values from 0 to 511; in each aligned block of 2048 rows (0 to 2047, 2048 to 4095, ...) at most 8 rows name the same one
- labels: int32 [262144], P(('dp', 'mp')), may hold values 0 or 1
- re_features: bfloat16 [262144, 256], P(('dp', 'mp')), may hold values from -6.5 to 6.5
- member_slot: int32 [512], replicated, may hold values from 0 to 511, each once
- coef: float32 [512, 256], P(('dp', 'mp')), may hold values from -0.9 to 0.9
Outputs:
- new_coef: float32 [512, 256], P(('dp', 'mp'))
- member_objective: float32 [512], P(('dp', 'mp'))
- new_margin: float32 [262144], P(('dp', 'mp'))
Inputs may be any that keep to these rules, and one draw needn't show every extreme that they name: `member_of`: among the rows of one device (aligned blocks of 2048 impressions) no member appears more than 8 times, and some member appears exactly 8 times in some blocks; every member appears somewhere. `member_slot` is a permutation; coefficient row m (the member whose member_slot is m) lives on device m // 4 of dp+mp.
All inputs are finite; a program needn't handle non-finite values. No bound on the sum of `labels` on one device may be relied on, other than what follows from the above.
Results may differ from a plain program's by a relative error of at most 0.0089.
Values may be sent and summed in bfloat16 or wider, within the bound.
A program may use at most 128 MiB of HBM per device.

v0:
```python
import jax
import jax.numpy as jnp
from jax import lax
from jax.sharding import PartitionSpec as P

R = 256
CAP = 8


LAMBDA = 1.0


def solve_one(factor, vector):
    return jax.scipy.linalg.cho_solve((factor, True), vector)


def shards(feat_values, feat_blocks, fixed_coef, member_of, labels, re_features, member_slot, coef):
    partial_value = jnp.sum(feat_values.astype(jnp.float32) * fixed_coef[feat_blocks], axis=(1, 2))
    fixed = lax.psum_scatter(partial_value, "mp", scatter_dimension=0, tiled=True)
    devices = lax.axis_size(("dp", "mp"))
    members = member_slot.shape[0]
    mem_dev = coef.shape[0]
    per_owner = mem_dev * CAP
    member = member_of[:, 0]
    row_count = member.shape[0]
    order = jnp.argsort(member, stable=True)
    ranked = member[order]
    place = jnp.arange(row_count, dtype=jnp.int32)
    changed = jnp.concatenate([jnp.ones((1,), bool), ranked[1:] != ranked[:-1]])
    first = lax.cummax(jnp.where(changed, place, 0), axis=0)
    rank = jnp.zeros((row_count,), jnp.int32).at[order].set(place - first)
    slot_of_row = member_slot[member]
    target = slot_of_row * CAP + rank
    owner = target // per_owner
    within = target % per_owner
    send_rows = jnp.zeros((members * CAP, R), jnp.bfloat16).at[target].set(re_features)
    send_rows = send_rows.reshape(devices, mem_dev, CAP, R)
    side_rows = jnp.stack(
        [fixed, labels.astype(jnp.float32), jnp.ones((row_count,), jnp.float32)], 1
    )
    send_side = (
        jnp.zeros((devices, 3, per_owner), jnp.float32)
        .at[owner[:, None], jnp.arange(3)[None, :], within[:, None]]
        .set(side_rows)
    )
    got_rows, got_side = (
        lax.all_to_all(
            send_rows.astype(jnp.float32), ("dp", "mp"), split_axis=0, concat_axis=0, tiled=True
        ).astype(send_rows.dtype),
        lax.all_to_all(send_side, ("dp", "mp"), split_axis=0, concat_axis=0, tiled=True),
    )
    side = got_side.reshape(devices, 3, mem_dev, CAP)
    got_fixed = side[:, 0]
    got_label = side[:, 1]
    live = side[:, 2]
    coef_b = coef.astype(jnp.bfloat16)
    score = got_fixed + jnp.einsum(
        "smcr,mr->smc", got_rows, coef_b, preferred_element_type=jnp.float32
    )
    probability = jax.nn.sigmoid(score)
    weight = live * probability * (1.0 - probability)
    residual = (live * (got_label - probability)).astype(jnp.bfloat16)
    weighted = (weight[..., None] * got_rows).astype(jnp.bfloat16)
    hessian = jnp.einsum("smcr,smcq->mrq", weighted, got_rows, preferred_element_type=jnp.float32)
    hessian = hessian + LAMBDA * jnp.eye(R, dtype=jnp.float32)
    gradient = (
        jnp.einsum("smc,smcr->mr", residual, got_rows, preferred_element_type=jnp.float32)
        - LAMBDA * coef
    )
    factor = jnp.linalg.cholesky(hessian)
    update = jax.vmap(solve_one)(factor, gradient)
    new_coef = coef + update
    logdet = 2.0 * jnp.sum(jnp.log(jnp.diagonal(factor, axis1=1, axis2=2)), axis=1)
    loglik = jnp.sum(live * (got_label * score - jax.nn.softplus(score)), axis=(0, 2))
    objective = loglik - 0.5 * LAMBDA * jnp.sum(coef * coef, axis=1) - 0.5 * logdet
    new_b = new_coef.astype(jnp.bfloat16)
    slot_margin = jnp.einsum("smcr,mr->smc", got_rows, new_b, preferred_element_type=jnp.float32)
    returned = lax.all_to_all(slot_margin, ("dp", "mp"), split_axis=0, concat_axis=0, tiled=True)
    random_part = returned.reshape(members * CAP)[target]
    return (new_coef, objective, fixed + random_part)


def solution(mesh):
    placed = (
        P("dp", "mp", None),
        P("dp", "mp"),
        P(),
        P(("dp", "mp"), None),
        P(("dp", "mp")),
        P(("dp", "mp"), None),
        P(),
        P(("dp", "mp"), None),
    )
    return jax.shard_map(
        shards,
        mesh=mesh,
        in_specs=placed,
        out_specs=(P(("dp", "mp"), None), P(("dp", "mp")), P(("dp", "mp"))),
        check_vma=False,
    )
```

profile of v0, /device:TPU:1, one launch (start us, length us, event | category | flops | bytes accessed | tf_op | source)
XLA Modules:
  0.0 566.8 jit_solution(15628420155218711525)
XLA Ops:
  2.1 5.7 %sort.17 = (s32[2048]{0:T(1024)}, s32[2048]{0:T(1024)S(1)}) sort(s32[2048]{0:T(1024)} %bitcast.158, s32[2048]{0:T(1024)S(1)} %iota.99), dimensions={0}, to_apply=%region_0.0 | sort | flops 22528 | bytes 32768 | tf_op jit(solution)/shard_map/jit(argsort)/sort | solution.py:26
  7.9 11.8 %gather_fusion.1 = s32[2048]{0:T(1024)S(1)} fusion(s32[2048]{0:T(1024)S(1)} %bitcast.159, s32[2048]{0:T(1024)S(1)} %get-tuple-element.38), kind=kCustom, calls=%fused_computation.1 | custom fusion | bytes 24576 | tf_op jit(solution)/shard_map/gather | solution.py:27
  20.5 13.2 %gather_fusion = s32[2048]{0:T(1024)S(1)} fusion(s32[512]{0:T(512)S(1)} %copy-done.2, s32[2048]{0:T(1024)S(1)} %broadcast_clamp_fusion.3), kind=kCustom, calls=%fused_computation | custom fusion | bytes 24576 | tf_op jit(solution)/shard_map/gather | solution.py:32
  33.7 8.0 %scatter_custom_fusion = s32[2048]{0:T(1024)S(1)} fusion(s32[2048]{0:T(1024)S(1)} %get-tuple-element.39, s32[2048]{0:T(1024)S(1)} %bitcast_subtract_fusion, s32[]{:T(128)} %copy.132), kind=kCustom, calls=%fused_computation.102 | custom fusion | bytes 8196 | tf_op jit(solution)/shard_map/scatter | solution.py:31
  43.8 2.6 copy.62
  46.5 4.0 reshape.152
  50.5 54.4 %gather_fusion.2 = f32[16384,128]{1,0:T(8,128)} fusion(f32[128,128]{1,0:T(8,128)S(1)} %copy-done, s32[16384]{0:T(1024)S(1)} %broadcast_clamp_fusion), kind=kCustom, calls=%fused_computation.2 | custom fusion | bytes 16842752 | tf_op jit(solution)/shard_map/gather | solution.py:18
  104.9 62.3 %multiply_reduce_fusion = f32[8192]{0:T(1024)S(1)} fusion(f32[8192,2,128]{2,1,0:T(2,128)} %bitcast.160, bf16[8192,2,128]{2,1,0:T(2,128)(2,1)} %param.8), kind=kLoop, calls=%fused_computation.10 | loop fusion | flops 6283264 | bytes 12615680 | tf_op jit(solution)/shard_map/reduce_sum | solution.py:18
  167.2 15.0 %all-reduce.1 = f32[8192]{0:T(1024)S(1)} all-reduce(f32[8192]{0:T(1024)S(1)} %multiply_reduce_fusion), channel_id=2, replica_groups=mesh['dp'=32,'mp'=4] {'mp'}, use_global_device_ids=true, to_apply=%region_5.6.clone | all-reduce | flops 8192 | bytes 65536
  184.7 23.0 %scatter_custom_fusion.2 = f32[12288]{0:T(1024)S(1)} fusion(s32[6144]{0:T(1024)S(1)} %reshape.188, f32[6144]{0:T(1024)S(1)} %reshape.190, f32[]{:T(128)} %constant.146.clone.1), kind=kCustom, calls=%fused_computation.56 | custom fusion | bytes 49156
  208.6 12.7 %all-to-all-start = ((f32[128,3,32]{2,1,0:T(4,128)}), f32[128,3,32]{2,1,0:T(4,128)S(1)}, u32[]{:S(2)}, u32[]{:S(2)}) async-start(f32[128,3,32]{2,1,0:T(4,128)} %copy.64), calls=%async_computation | async-start | bytes 524288 | tf_op jit(solution)/shard_map/all_to_all | solution.py:50
  221.2 11.3 %scatter_custom_fusion.1 = bf16[4096,256]{1,0:T(8,128)(2,1)} fusion(s32[2048]{0:T(1024)S(1)} %get-tuple-element.36, bf16[2048,256]{1,0:T(8,128)(2,1)} %param.13, bf16[]{:T(256)} %constant.160.clone.1), kind=kCustom, calls=%fused_computation.22 | custom fusion | bytes 2097664 | tf_op jit(solution)/shard_map/scatter | solution.py:36
  232.5 10.0 %all-to-all-start.1 = ((bf16[128,4,8,256]{3,2,1,0:T(8,128)(2,1)}), bf16[128,4,8,256]{3,2,1,0:T(8,128)(2,1)S(1)}, u32[]{:S(2)}, u32[]{:S(2)}) async-start(bf16[128,4,8,256]{3,2,1,0:T(8,128)(2,1)} %bitcast.162), calls=%async_computation.1 | async-start | bytes 4194304 | tf_op jit(solution)/shard_map/all_to_all | solution.py:47
  244.6 28.4 %all-to-all-done.1 = bf16[128,4,8,256]{3,2,1,0:T(8,128)(2,1)S(1)} async-done(((bf16[128,4,8,256]{3,2,1,0:T(8,128)(2,1)}), bf16[128,4,8,256]{3,2,1,0:T(8,128)(2,1)S(1)}, u32[]{:S(2)}, u32[]{:S(2)}) %all-to-all-start.1) | async-done | bytes 2097184 | tf_op jit(solution)/shard_map/all_to_all | solution.py:47
  273.0 2.3 fusion.34
  276.1 2.3 fusion.25
  278.5 5.4 fusion.2
  287.7 46.9 %custom-call.20 = f32[4,128,128]{2,1,0:T(8,128)S(1)} custom-call(f32[4,128,128]{2,1,0:T(8,128)S(1)} %cholesky.122), custom_call_target="Cholesky" | custom-call | tf_op jit(solution)/shard_map/jit(cholesky)/cholesky | solution.py:70
  335.5 40.9 %custom-call.21 = f32[4,1,128,128]{2,3,1,0:T(8,128)} custom-call(f32[4,1,128,128]{3,2,1,0:T(8,128)} %select_bitcast_fusion), custom_call_target="InvertDiagBlocksLowerTriangular" | custom-call | tf_op jit(solution)/shard_map/jit(cholesky)/cholesky | solution.py:70
  377.8 2.3 convolution_subtract_fusion
  380.2 48.4 %custom-call.22 = f32[4,128,128]{2,1,0:T(8,128)} custom-call(f32[4,128,128]{2,1,0:T(8,128)} %convolution_subtract_fusion), custom_call_target="Cholesky" | custom-call | tf_op jit(solution)/shard_map/jit(cholesky)/cholesky | solution.py:70
  430.5 2.5 broadcast_select_fusion
  433.0 5.4 while.1
  433.6 2.1 bitcast_dynamic-update-slice_fusion.2
  436.3 2.1 bitcast_dynamic-update-slice_fusion.2
  438.5 80.3 %custom-call.23 = f32[4,2,128,128]{2,3,1,0:T(8,128)} custom-call(f32[4,2,128,128]{3,2,1,0:T(8,128)} %bitcast.177), custom_call_target="InvertDiagBlocksLowerTriangular" | custom-call | tf_op jit(solution)/shard_map/vmap(jit(_cho_solve))/triangular_solve | solution.py:14
  523.7 1.5 fusion.12
  525.8 2.3 fusion.32
  528.9 3.8 all-to-all-start.2
  532.7 17.4 %copy.72 = f32[4,256,256]{0,2,1:T(8,128)} copy(f32[4,256,256]{2,1,0:T(8,128)} %get-tuple-element.28) | data formatting | bytes 2097152 | tf_op jit(solution)/shard_map/jit(cholesky)/select_n | solution.py:70
  550.1 2.3 gather_fusion.3
  553.3 11.8 %gather_fusion.4 = f32[2048]{0:T(1024)S(1)} fusion(f32[4096]{0:T(1024)S(1)} %reshape.107, s32[2048]{0:T(1024)S(1)} %copy-done.10), kind=kCustom, calls=%fused_computation.4 | custom fusion | bytes 24576 | tf_op jit(solution)/shard_map/gather | solution.py:79
  (105 shorter events, 27.6 us)
Async XLA Ops:
  0.6 49.9 %copy-start = (f32[128,128]{1,0:T(8,128)S(1)}, f32[128,128]{1,0:T(8,128)}, u32[]{:S(2)}) copy-start(f32[128,128]{1,0:T(8,128)} %param.10) | copy-start | bytes 196612
  0.6 7.2 %copy-start.3 = (s32[2048,1]{0,1:T(1,128)S(1)}, s32[2048,1]{0,1:T(1,128)}, u32[]{:S(2)}) copy-start(s32[2048,1]{0,1:T(1,128)} %param.11) | copy-start | bytes 24580
  19.7 0.8 copy-start.2
  20.4 22.0 %copy-start.13 = (s32[3]{0:T(128)S(1)}, s32[3]{0:T(128)}, u32[]{:S(2)}) copy-start(s32[3]{0:T(128)} %constant.173) | copy-start | bytes 40
  20.4 22.2 %copy-start.12 = (s32[3]{0:T(128)S(1)}, s32[3]{0:T(128)}, u32[]{:S(2)}) copy-start(s32[3]{0:T(128)} %constant.170) | copy-start | bytes 40
  20.4 22.3 %copy-start.8 = (s32[8192,2]{0,1:T(2,128)S(1)}, s32[8192,2]{0,1:T(2,128)}, u32[]{:S(2)}) copy-start(s32[8192,2]{0,1:T(2,128)} %param.9) | copy-start | bytes 196612
  104.9 77.3 %copy-start.14 = (u32[128]{0:T(128)S(1)}, u32[128]{0:T(128)}, u32[]{:S(2)}) copy-start(u32[128]{0:T(128)} %constant.208) | copy-start | bytes 1540
  182.2 1.8 copy-start.6
  208.6 24.0 %all-to-all-start = ((f32[128,3,32]{2,1,0:T(4,128)}), f32[128,3,32]{2,1,0:T(4,128)S(1)}, u32[]{:S(2)}, u32[]{:S(2)}) async-start(f32[128,3,32]{2,1,0:T(4,128)} %copy.64), calls=%async_computation | async-start | bytes 524288 | tf_op jit(solution)/shard_map/all_to_all | solution.py:50
  232.5 12.0 %copy-start.9 = (f32[4,256]{1,0:T(4,128)S(1)}, f32[4,256]{1,0:T(4,128)}, u32[]{:S(2)}) copy-start(f32[4,256]{1,0:T(4,128)} %param.15) | copy-start | bytes 12292
  232.5 40.5 %all-to-all-start.1 = ((bf16[128,4,8,256]{3,2,1,0:T(8,128)(2,1)}), bf16[128,4,8,256]{3,2,1,0:T(8,128)(2,1)S(1)}, u32[]{:S(2)}, u32[]{:S(2)}) async-start(bf16[128,4,8,256]{3,2,1,0:T(8,128)(2,1)} %bitcast.162), calls=%async_computation.1 | async-start | bytes 4194304 | tf_op jit(solution)/shard_map/all_to_all | solution.py:47
  285.2 49.5 %copy-start.7 = (pred[128,128]{1,0:T(8,128)(4,1)S(1)}, pred[128,128]{1,0:T(8,128)(4,1)}, u32[]{:S(2)}) copy-start(pred[128,128]{1,0:T(8,128)(4,1)} %iota_compare_fusion.3) | copy-start | bytes 49156
  286.7 1.0 copy-start.5
  380.2 52.8 %copy-start.15 = (s32[2]{0:T(128)S(1)}, s32[2]{0:T(128)}, u32[]{:S(2)}) copy-start(s32[2]{0:T(128)} %iota_multiply_fusion) | copy-start | bytes 28
  429.5 1.0 copy-start.4
  528.9 24.1 %all-to-all-start.2 = ((f32[128,4,8]{2,1,0:T(4,128)}), f32[128,4,8]{2,1,0:T(4,128)S(1)}, u32[]{:S(2)}, u32[]{:S(2)}) async-start(f32[128,4,8]{2,1,0:T(4,128)} %bitcast.59), calls=%async_computation.2 | async-start | bytes 524288 | tf_op jit(solution)/shard_map/all_to_all | solution.py:78
  532.7 19.8 %copy-start.11 = (f32[4]{0:T(128)S(1)}, f32[4]{0:T(128)}, u32[]{:S(2)}) copy-start(f32[4]{0:T(128)} %get-tuple-element.32) | copy-start | bytes 52
  532.7 20.6 %copy-start.10 = (s32[2048]{0:T(1024)S(1)}, s32[2048]{0:T(1024)}, u32[]{:S(2)}) copy-start(s32[2048]{0:T(1024)} %get-tuple-element.23) | copy-start | bytes 24580
  553.3 13.1 %copy-start.1 = (f32[128,128]{1,0:T(8,128)S(1)}, f32[128,128]{1,0:T(8,128)}, u32[]{:S(2)}) copy-start(f32[128,128]{1,0:T(8,128)} %param.10) | copy-start | bytes 196612
where the time goes:
time: 576 us; the launch traced here: 567 us
  other arithmetic  299 us (52%)
  local copies, waits for them, and re-layouts  174 us (30%)
  waiting for transfers between devices  28.4 us (5%)
  starting transfers between devices  26.5 us (5%)
  matrix products  22.5 us (4%)
  blocking collectives  15 us (3%)
    another operation x10, other arithmetic, shards(): factor = jnp.linalg.cholesky(hessian)  139 us
    another operation x6, other arithmetic, solve_one(): return jax.scipy.linalg.cho_solve((factor, True), vector)  83.3 us
    reduce_sum x1, other arithmetic, shards(): jnp.sum(feat_values.astype(jnp.float32) * fixed_coef[feat_blocks], axis=(...  62.3 us
    gather x1, local copies, waits for them, and re-layouts, shards(): fixed_coef[feat_blocks]  54.4 us
    all_to_all x1, waiting for transfers between devices, shards(): lax.all_to_all(send_rows.astype(jnp.float32), ('dp', 'mp'), split_axis=0,...  28.4 us
    unnamed x37, local copies, waits for them, and re-layouts  26.4 us
    select_n x1, local copies, waits for them, and re-layouts, shards(): factor = jnp.linalg.cholesky(hessian)  17.4 us
    unnamed x1, blocking collectives  15 us
  transfers between devices with their start and end apart: 3, of which 1 were waited for; matrix products, arithmetic and copies ran while one was open for 6% of the time, Pallas kernels for 0%

commit v1 on v0

v1 whole, which is shorter than its diff:
```python
import functools

import jax
import jax.numpy as jnp
from jax import lax
from jax.experimental import pallas as pl
from jax.experimental.pallas import tpu as pltpu
from jax.sharding import PartitionSpec as P

R = 256
CAP = 8
LAMBDA = 1.0

MESH = pl.DeviceIdType.MESH
F32 = jnp.float32
BF16 = jnp.bfloat16
NT = (((1,), (1,)), ((), ()))
TN = (((0,), (0,)), ((), ()))
MIB = 1 << 20


def iota(shape, axis):
    return lax.broadcasted_iota(jnp.int32, shape, axis)


def halves(x):
    high = x.astype(BF16)
    return high, (x - high.astype(F32)).astype(BF16)


def thirds(x):
    high, rest = x.astype(BF16), None
    rest = x - high.astype(F32)
    middle = rest.astype(BF16)
    return high, middle, (rest - middle.astype(F32)).astype(BF16)


def place(device):
    return (device // 4, lax.rem(device, 4))


def position():
    return lax.axis_index("dp") * 4 + lax.axis_index("mp")


def one_hot(condition):
    return jnp.where(condition, 1.0, 0.0).astype(BF16)


def ring_peers(me):
    inner, outer = lax.rem(me, 8), me // 8
    first = [outer * 8 + lax.rem(inner + k, 8) for k in range(1, 8)]
    x, z = lax.rem(outer, 4), outer // 4
    second = [(z * 4 + lax.rem(x + k, 4)) * 8 + inner for k in range(1, 4)]
    third = [(lax.rem(z + k, 4) * 4 + x) * 8 + inner for k in range(1, 4)]
    return first, second, third


def gather_stage(table, me, stage, send_sem, recv_sem):
    peers = ring_peers(me)[stage]
    rows = (8, 64, 256)[stage]
    block = pl.ds(pl.multiple_of((me * 8) // rows * rows, rows), rows)
    for peer in peers:
        pltpu.make_async_remote_copy(
            src_ref=table.at[block],
            dst_ref=table.at[block],
            send_sem=send_sem.at[stage],
            recv_sem=recv_sem.at[stage],
            device_id=place(peer),
            device_id_type=MESH,
        ).start()

    def finish():
        whole = table.at[pl.ds(0, rows * len(peers))]
        waiting = pltpu.make_async_remote_copy(
            src_ref=whole,
            dst_ref=whole,
            send_sem=send_sem.at[stage],
            recv_sem=recv_sem.at[stage],
            device_id=place(peers[0]),
            device_id_type=MESH,
        )
        waiting.wait_send()
        waiting.wait_recv()

    return finish


def row_products(table, z_ref, slot_ref, out_ref):
    half = [table[pl.ds(h, 512, stride=2), :].astype(BF16) for h in range(2)]
    coefs = jnp.concatenate(half, axis=1)
    for c in range(8):
        lanes = pl.ds(256 * c, 256)
        product = lax.dot_general(coefs, z_ref[lanes, :], NT, preferred_element_type=F32)
        chosen = iota((512, 256), 0) == slot_ref[:, lanes]
        out_ref[:, lanes] = jnp.sum(jnp.where(chosen, product, 0.0), axis=0, keepdims=True)


def dispatch_kernel(
    v_ref, ids_ref, w_ref, member_ref, label_ref, z_ref, slots_ref, coef_ref,
    hess_ref, grad_ref, side_sum_ref, slot_ref, fixed_ref,
    onehot, ids2, part, fixed_part, fixed_recv, table, target_ref, score_ref,
    send, recv, side_send, side_recv,
    send_sem, recv_sem, table_send_sem, table_recv_sem,
):
    me = position()
    mine = lax.axis_index("mp")

    barrier = pltpu.get_barrier_semaphore()

    def greet(k, carry):
        peer = lax.rem(me + k, 128)
        pl.semaphore_signal(barrier, inc=1, device_id=place(peer), device_id_type=MESH)
        return carry

    lax.fori_loop(1, 128, greet, 0)
    table[pl.ds(pl.multiple_of(me * 8, 8), 8), :] = coef_ref[...]

    for c in range(8):
        lanes = pl.ds(256 * c, 256)
        onehot[:, lanes] = one_hot(iota((512, 256), 0) == member_ref[:, lanes])
    slots = slots_ref[...]
    sub = iota((8, 512), 0)
    owner_row = jnp.where(sub == 0, slots // 4, jnp.where(sub == 1, lax.rem(slots, 4), 0))
    owner_row = owner_row.astype(F32).astype(BF16)
    before = one_hot(iota((256, 256), 0) < iota((256, 256), 1))
    tally = jnp.concatenate([before, jnp.ones((256, 256), BF16)], axis=1)
    base = jnp.zeros((512, 256), F32)
    for c in range(8):
        lanes = pl.ds(256 * c, 256)
        hot = onehot[:, lanes]
        found = jnp.dot(owner_row, hot, preferred_element_type=F32)
        counted = jnp.dot(hot, tally, preferred_element_type=F32)
        rank = jnp.sum(hot.astype(F32) * (base + counted[:, :256]), axis=0, keepdims=True)
        base = base + counted[:, 256:]
        slot = found[0:1] * 4.0 + found[1:2]
        slot_ref[:, lanes] = slot.astype(jnp.int32)
        target_ref[:, lanes] = (slot * 8.0 + rank).astype(jnp.int32)

    pl.semaphore_wait(barrier, 127)
    finish_first = gather_stage(table, me, 0, table_send_sem, table_recv_sem)

    for r in range(64):
        for k in range(2):
            ids2[k, r:r + 1, :] = ids_ref[k:k + 1, 128 * r:128 * r + 128]
    spread = [one_hot(iota((128, 256), 1) == 2 * iota((128, 256), 0) + k) for k in range(2)]
    ids = sum(
        jnp.dot(ids2[k].astype(F32).astype(BF16), spread[k], preferred_element_type=F32)
        for k in range(2)
    )
    part[...] = ids
    w2 = jnp.concatenate(halves(w_ref[...]), axis=1)

    def margin_rows(r, carry):
        rows = v_ref[pl.ds(pl.multiple_of(r * 256, 256), 256), :]
        product = lax.dot_general(
            w2, jnp.concatenate([rows, rows], axis=1), NT, preferred_element_type=F32
        )
        chosen = iota((128, 256), 0) == part[pl.ds(r, 1), :].astype(jnp.int32)
        part[pl.ds(r, 1), :] = jnp.sum(jnp.where(chosen, product, 0.0), axis=0, keepdims=True)
        return carry

    lax.fori_loop(0, 64, margin_rows, 0, unroll=4)
    pairs = one_hot(iota((256, 128), 0) // 2 == iota((256, 128), 1))
    fixed_part[...] = sum(
        jnp.dot(piece, pairs, preferred_element_type=F32) for piece in thirds(part[...])
    )
    for k in range(1, 4):
        other = lax.rem(mine + k, 4)
        pltpu.make_async_remote_copy(
            src_ref=fixed_part.at[pl.ds(pl.multiple_of(other * 16, 16), 16)],
            dst_ref=fixed_recv.at[pl.ds(k * 16, 16)],
            send_sem=send_sem.at[0],
            recv_sem=recv_sem.at[0],
            device_id=(lax.axis_index("dp"), other),
            device_id_type=MESH,
        ).start()

    finish_first()
    finish_second = gather_stage(table, me, 1, table_send_sem, table_recv_sem)

    waiting = pltpu.make_async_remote_copy(
        src_ref=fixed_part.at[pl.ds(0, 48)],
        dst_ref=fixed_recv.at[pl.ds(16, 48)],
        send_sem=send_sem.at[0],
        recv_sem=recv_sem.at[0],
        device_id=(lax.axis_index("dp"), mine),
        device_id_type=MESH,
    )
    waiting.wait_send()
    waiting.wait_recv()
    own = fixed_part[pl.ds(pl.multiple_of(mine * 16, 16), 16), :]
    total = own + fixed_recv[16:32] + fixed_recv[32:48] + fixed_recv[48:64]
    for r in range(16):
        fixed_ref[:, 128 * r:128 * r + 128] = total[r:r + 1, :]

    finish_second()
    finish_third = gather_stage(table, me, 2, table_send_sem, table_recv_sem)

    def send_rows(c, carry):
        chunk = lax.rem(me // 8 + c, 16)
        target = target_ref[...] - chunk * 256
        picked = jnp.zeros((256, 256), F32)
        for piece in range(4):
            lanes = pl.ds(512 * piece, 512)
            hot = one_hot(iota((256, 512), 0) == target[:, 512 * piece:512 * piece + 512])
            picked = picked + jnp.dot(hot, z_ref[lanes, :], preferred_element_type=F32)
        send[pl.ds(chunk * 8, 8)] = picked.astype(BF16).reshape(8, 32, 256)

        def send_one(j, inner):
            owner = chunk * 8 + lax.rem(me + j, 8)

            @pl.when(owner != me)
            def _():
                pltpu.make_async_remote_copy(
                    src_ref=send.at[owner],
                    dst_ref=recv.at[me],
                    send_sem=send_sem.at[1],
                    recv_sem=recv_sem.at[1],
                    device_id=place(owner),
                    device_id_type=MESH,
                ).start()

            return inner

        return lax.fori_loop(0, 8, send_one, carry)

    lax.fori_loop(0, 16, send_rows, 0)
    recv[pl.ds(me, 1)] = send[pl.ds(me, 1)]

    finish_third()
    row_products(table, z_ref, slot_ref, score_ref)
    score = score_ref[...] + fixed_ref[...]
    label = label_ref[...].astype(F32)
    small = jnp.exp(-jnp.abs(score))
    probability = jnp.where(score >= 0.0, 1.0, small) / (1.0 + small)
    weight = small / ((1.0 + small) * (1.0 + small))
    residual = label - probability
    likelihood = label * score - (jnp.maximum(score, 0.0) + jnp.log1p(small))
    target = target_ref[...]
    total_side = jnp.zeros((128, 128), F32)
    for c in range(4):
        lanes = slice(512 * c, 512 * c + 512)
        owner_hot = one_hot(iota((128, 512), 0) == target[:, lanes] // 32)
        within = iota((32, 512), 0) == lax.rem(target[:, lanes], 32)
        sides = jnp.concatenate(
            [jnp.where(within, q[:, lanes], 0.0) for q in (weight, residual, likelihood)]
            + [jnp.zeros((32, 512), F32)],
            axis=0,
        )
        for piece in halves(sides):
            total_side = total_side + lax.dot_general(
                owner_hot, piece, NT, preferred_element_type=F32
            )
    for d in range(128):
        side_send[d] = total_side[d:d + 1, :]

    def send_side(k, carry):
        owner = lax.rem(me + k, 128)
        pltpu.make_async_remote_copy(
            src_ref=side_send.at[owner],
            dst_ref=side_recv.at[me],
            send_sem=send_sem.at[2],
            recv_sem=recv_sem.at[2],
            device_id=place(owner),
            device_id_type=MESH,
        ).start()
        return carry

    lax.fori_loop(1, 128, send_side, 0)
    side_recv[pl.ds(me, 1)] = side_send[pl.ds(me, 1)]

    for number, sent, got in ((1, send, recv), (2, side_send, side_recv)):
        waiting = pltpu.make_async_remote_copy(
            src_ref=sent.at[pl.ds(0, 127)],
            dst_ref=got.at[pl.ds(0, 127)],
            send_sem=send_sem.at[number],
            recv_sem=recv_sem.at[number],
            device_id=place(me),
            device_id_type=MESH,
        )
        waiting.wait_send()
        waiting.wait_recv()

    side_sum_ref[...] = jnp.sum(side_recv[...], axis=0)
    eye = jnp.where(iota((256, 256), 0) == iota((256, 256), 1), LAMBDA, 0.0)
    for m in range(4):
        hess_ref[m] = eye
    grad_ref[...] = jnp.zeros((4, 8, 256), F32)
    ones = jnp.ones((256, 128), BF16)

    def accumulate(c, carry):
        sources = pl.ds(pl.multiple_of(c * 32, 32), 32)
        sides = jnp.broadcast_to(side_recv[sources], (32, 8, 128))
        lane = iota((32, 8, 128), 2) - iota((32, 8, 128), 1)
        for m in range(4):
            rows = recv[sources, 8 * m:8 * m + 8, :].astype(F32).reshape(256, 256)
            rows_b = rows.astype(BF16)
            column = []
            for quantity in range(2):
                chosen = lane == 32 * quantity + 8 * m
                picked = jnp.where(chosen, sides, 0.0).reshape(256, 128)
                picked = jnp.concatenate(halves(picked), axis=1)
                column.append(jnp.dot(picked, ones, preferred_element_type=F32))
            weights = jnp.concatenate([column[0], column[0]], axis=1)
            weighted = (weights * rows).astype(BF16)
            hess_ref[m] += lax.dot_general(weighted, rows_b, TN, preferred_element_type=F32)
            pull = lax.dot_general(
                column[1].astype(BF16), rows_b, TN, preferred_element_type=F32
            )
            grad_ref[m] += pull[0:8]
        return carry

    lax.fori_loop(0, 4, accumulate, 0)


def dispatch(v, ids, fixed_coef, member, labels, z, slots, coef8):
    vmem = pl.BlockSpec(memory_space=pltpu.VMEM)
    return pl.pallas_call(
        dispatch_kernel,
        out_shape=(
            jax.ShapeDtypeStruct((4, 256, 256), F32),
            jax.ShapeDtypeStruct((4, 8, 256), F32),
            jax.ShapeDtypeStruct((1, 128), F32),
            jax.ShapeDtypeStruct((1, 2048), jnp.int32),
            jax.ShapeDtypeStruct((1, 2048), F32),
        ),
        in_specs=[vmem] * 8,
        out_specs=(vmem,) * 5,
        scratch_shapes=[
            pltpu.VMEM((512, 2048), BF16),
            pltpu.VMEM((2, 64, 128), jnp.int32),
            pltpu.VMEM((64, 256), F32),
            pltpu.VMEM((64, 128), F32),
            pltpu.VMEM((64, 128), F32),
            pltpu.VMEM((1024, 128), F32),
            pltpu.VMEM((1, 2048), jnp.int32),
            pltpu.VMEM((1, 2048), F32),
            pltpu.VMEM((128, 32, 256), BF16),
            pltpu.VMEM((128, 32, 256), BF16),
            pltpu.VMEM((128, 1, 128), F32),
            pltpu.VMEM((128, 1, 128), F32),
            pltpu.SemaphoreType.DMA((3,)),
            pltpu.SemaphoreType.DMA((3,)),
            pltpu.SemaphoreType.DMA((3,)),
            pltpu.SemaphoreType.DMA((3,)),
        ],
        compiler_params=pltpu.CompilerParams(
            collective_id=0, has_side_effects=True, vmem_limit_bytes=48 * MIB
        ),
        name="dispatch",
    )(v, ids, fixed_coef, member, labels, z, slots, coef8)


def dot6(left, right, dims):
    lh, lm, ll = thirds(left)
    rh, rm, rl = thirds(right)
    ((la,), (ra,)), _ = dims
    return lax.dot_general(
        jnp.concatenate([lh, lh, lm, lm, lh, ll], axis=la),
        jnp.concatenate([rh, rm, rh, rm, rl, rh], axis=ra),
        dims,
        preferred_element_type=F32,
    )


def invert_packed(packed, pivots, first):
    lane = iota((32, 128), 1)
    group = lane // 32 * 32
    local = lane - group
    sub = iota((32, 128), 0)
    for j in range(32):
        column = jnp.take_along_axis(packed, group + j, axis=1, mode="promise_in_bounds")
        row = jnp.broadcast_to(packed[j:j + 1], (32, 128))
        pivot = jnp.broadcast_to(column[j:j + 1], (32, 128))
        pivots[first + j:first + j + 1, :] = column[j:j + 1]
        inverse = 1.0 / pivot
        at = local == j
        row = jnp.where(at, inverse, row * inverse)
        packed = jnp.where(sub == j, row, jnp.where(at, 0.0, packed) - column * row)
    return packed


def solve_kernel(hess_ref, grad_ref, side_ref, coef_ref, new_ref, objective_ref, a_ref, pivots):
    lane = iota((1, 256), 1)
    for m in range(4):
        one_sided = hess_ref[m]
        a_ref[m] = 0.5 * (one_sided + one_sided.T)
    for k in range(8):
        low = 32 * k
        blocks = [a_ref[m, low:low + 32, :] for m in range(4)]
        packed = jnp.concatenate([b[:, low:low + 32] for b in blocks], axis=1)
        inverse = invert_packed(packed, pivots, low)
        inside = (lane >= low) & (lane < low + 32)
        sign = jnp.where(lane < low, -1.0, 1.0)
        for m in range(4):
            own = inverse[:, 32 * m:32 * m + 32]
            wide = jnp.concatenate(
                ([jnp.zeros((32, low), F32)] if low else []) + [own]
                + ([jnp.zeros((32, 224 - low), F32)] if low < 224 else []),
                axis=1,
            )
            right = jnp.where(inside, wide, dot6(own, blocks[m], (((1,), (0,)), ((), ()))))
            change = dot6(blocks[m] * sign, right, TN)
            a_ref[m] = jnp.where(inside, 0.0, a_ref[m]) - change
            a_ref[m, low:low + 32, :] = right
    logs = jnp.sum(jnp.log(pivots[...]), axis=0, keepdims=True)
    side_lane = iota((1, 128), 1)
    for m in range(4):
        coef = coef_ref[m:m + 1, :]
        gradient = grad_ref[m] - LAMBDA * coef
        update = dot6(gradient, a_ref[m], (((1,), (0,)), ((), ())))
        new_ref[m:m + 1, :] = coef + update[0:1]
        half_logdet = 0.5 * jnp.sum(jnp.where(side_lane == 32 * m, logs, 0.0))
        mine = (side_lane >= 64 + 8 * m) & (side_lane < 72 + 8 * m)
        likelihood = jnp.sum(jnp.where(mine, side_ref[...], 0.0))
        objective_ref[m] = likelihood - 0.5 * LAMBDA * jnp.sum(coef * coef) - half_logdet


def solve(hess, grad, side_sum, coef):
    vmem = pl.BlockSpec(memory_space=pltpu.VMEM)
    return pl.pallas_call(
        solve_kernel,
        out_shape=(jax.ShapeDtypeStruct((4, 256), F32), jax.ShapeDtypeStruct((4,), F32)),
        in_specs=[vmem] * 4,
        out_specs=(vmem, pl.BlockSpec(memory_space=pltpu.SMEM)),
        scratch_shapes=[pltpu.VMEM((4, 256, 256), F32), pltpu.VMEM((256, 128), F32)],
        compiler_params=pltpu.CompilerParams(vmem_limit_bytes=32 * MIB),
        name="newton",
    )(hess, grad, side_sum, coef)


def margin_kernel(new_ref, z_ref, slot_ref, fixed_ref, out_ref, table, send_sem, recv_sem):
    me = position()
    barrier = pltpu.get_barrier_semaphore()
    peers = sum(ring_peers(me), [])
    for peer in peers:
        pl.semaphore_signal(barrier, inc=1, device_id=place(peer), device_id_type=MESH)
    table[pl.ds(pl.multiple_of(me * 8, 8), 8), :] = new_ref[...]
    pl.semaphore_wait(barrier, len(peers))
    for stage in range(3):
        gather_stage(table, me, stage, send_sem, recv_sem)()
    row_products(table, z_ref, slot_ref, out_ref)
    out_ref[...] += fixed_ref[...]


def margins(new8, z, slot, fixed):
    vmem = pl.BlockSpec(memory_space=pltpu.VMEM)
    return pl.pallas_call(
        margin_kernel,
        out_shape=jax.ShapeDtypeStruct((1, 2048), F32),
        in_specs=[vmem] * 4,
        out_specs=vmem,
        scratch_shapes=[
            pltpu.VMEM((1024, 128), F32),
            pltpu.SemaphoreType.DMA((3,)),
            pltpu.SemaphoreType.DMA((3,)),
        ],
        compiler_params=pltpu.CompilerParams(
            collective_id=1, has_side_effects=True, vmem_limit_bytes=32 * MIB
        ),
        name="margins",
    )(new8, z, slot, fixed)


def shards(feat_values, feat_blocks, fixed_coef, member_of, labels, re_features, member_slot, coef):
    hess, grad, side_sum, slot, fixed = dispatch(
        feat_values.reshape(16384, 128),
        feat_blocks.T,
        fixed_coef,
        member_of.reshape(1, 2048),
        labels.reshape(1, 2048),
        re_features,
        member_slot.reshape(1, 512),
        coef.reshape(8, 128),
    )
    new_coef, objective = solve(hess, grad, side_sum, coef)
    margin = margins(new_coef.reshape(8, 128), re_features, slot, fixed)
    return (new_coef, objective, margin.reshape(2048))


def solution(mesh):
    placed = (
        P("dp", "mp", None),
        P("dp", "mp"),
        P(),
        P(("dp", "mp"), None),
        P(("dp", "mp")),
        P(("dp", "mp"), None),
        P(),
        P(("dp", "mp"), None),
    )
    return jax.shard_map(
        shards,
        mesh=mesh,
        in_specs=placed,
        out_specs=(P(("dp", "mp"), None), P(("dp", "mp")), P(("dp", "mp"))),
        check_vma=False,
    )
```

time: 576 us -> 122 us (0.21); the launches traced: 567 us -> 120 us
  other arithmetic: 299 us -> 0 us
  local copies, waits for them, and re-layouts: 174 us -> 7.04 us
  Pallas kernels: 0 us -> 112 us
  waiting for transfers between devices: 28.4 us -> 0 us
  starting transfers between devices: 26.5 us -> 0 us
  matrix products: 22.5 us -> 0 us
  blocking collectives: 15 us -> 0 us
    another operation x19 -> x0, other arithmetic: 222 us -> none  [the longest x10 139 us: shards(): factor = jnp.linalg.cholesky(hessian)]
    pallas_call x0 -> x3, Pallas kernels: none -> 112 us  [the longest x1 67.8 us: dispatch(): pl.pallas_call(dispatch_kernel, out_shape=(jax.ShapeDtypeStruct((4, 256,...]
    gather x5 -> x0, local copies, waits for them, and re-layouts: 93.5 us -> none  [the longest x1 54.4 us: shards(): fixed_coef[feat_blocks]]
    reduce_sum x4 -> x0, other arithmetic: 63.2 us -> none  [the longest x1 62.3 us: shards(): jnp.sum(feat_values.astype(jnp.float32) * fixed_coef[feat_blocks], axis=(...]
    all_to_all x3 -> x0, waiting for transfers between devices: 28.4 us -> none  [the longest x1 28.4 us: shards(): lax.all_to_all(send_rows.astype(jnp.float32), ('dp', 'mp'), split_axis=0,...]
    all_to_all x3 -> x0, starting transfers between devices: 26.5 us -> none  [the longest x1 12.7 us: shards(): lax.all_to_all(send_side, ('dp', 'mp'), split_axis=0, concat_axis=0, tile...]
    unnamed x37 -> x17, local copies, waits for them, and re-layouts: 26.4 us -> 5.58 us
    scatter x3 -> x0, local copies, waits for them, and re-layouts: 20.2 us -> none  [the longest x1 11.3 us: shards(): jnp.zeros((members * CAP, R), jnp.bfloat16).at[target].set(re_features)]
  transfers between devices with their start and end apart: 3 -> 0, of which waited for: 1 -> 0; matrix products, arithmetic and copies ran while one was open for 6% -> 0% of each run, Pallas kernels for 0% -> 0%
where the time goes in v1:
time: 122 us; the launch traced here: 120 us
  Pallas kernels  112 us (92%)
  local copies, waits for them, and re-layouts  7.04 us (6%)
    pallas_call x1, Pallas kernels, dispatch(): pl.pallas_call(dispatch_kernel, out_shape=(jax.ShapeDtypeStruct((4, 256,...  67.8 us
    pallas_call x1, Pallas kernels, solve(): pl.pallas_call(solve_kernel, out_shape=(jax.ShapeDtypeStruct((4, 256), F3...  28.5 us
    pallas_call x1, Pallas kernels, margins(): pl.pallas_call(margin_kernel, out_shape=jax.ShapeDtypeStruct((1, 2048), F...  16 us
    unnamed x17, local copies, waits for them, and re-layouts  5.58 us

profile of v1, /device:TPU:1, one launch (start us, length us, event | category | flops | bytes accessed | tf_op | source)
XLA Modules:
  0.0 120.0 jit_solution(12557765314670536516)
XLA Ops:
  0.6 0.0 copy-start.4
  0.6 0.8 reshape.31.coef_ref
  1.4 0.0 copy-start
  1.4 1.2 %copy-done = bf16[2048,256]{1,0:T(8,128)(2,1)S(1)} copy-done((bf16[2048,256]{1,0:T(8,128)(2,1)S(1)}, bf16[2048,256]{1,0:T(8,128)(2,1)}, u32[]{:S(2)}) %copy-start) | copy-done | bytes 1048600
  2.6 0.0 copy-start.2
  2.6 0.8 copy-done.2
  3.5 0.0 copy-start.3
  3.5 0.8 copy-done.3
  4.3 0.0 copy-start.5
  4.3 0.7 copy-done.5
  5.0 0.0 copy-start.6
  5.0 0.7 copy-done.6
  5.7 0.0 copy-start.7
  5.7 0.7 copy-done.7
  6.4 0.0 copy-start.1
  6.4 67.8 %dispatch.1 = (f32[4,256,256]{2,1,0:T(8,128)S(1)}, f32[4,8,256]{2,1,0:T(8,128)S(1)}, f32[1,128]{1,0:T(1,128)S(1)}, s32[1,2048]{1,0:T(1,128)S(1)}, f32[1,2048]{1,0:T(1,128)S(1)}) custom-call(bf16[16384,128]{1,0:T(8,128)(2,1)} %bitcast.11, s32[2,8192]{1,0:T(2,128)S(1)} %bitcast.6, f32[128,128]{1,0:T(8,128)S(1)} %copy-done.3, s32[1,2048]{1,0:T(1,128)S(1)} %bitcast.8, ...), custom_call_target="tpu_custom_call" | custom-call | tf_op jit(solution)/shard_map/dispatch/pallas_call | solution.py:319
  74.2 0.0 copy-done.4
  74.2 28.5 %newton.1 = (f32[4,256]{1,0:T(4,128)}, f32[4]{0:T(128)}) custom-call(f32[4,256,256]{2,1,0:T(8,128)S(1)} %get-tuple-element.10.hess_ref, f32[4,8,256]{2,1,0:T(8,128)S(1)} %get-tuple-element.11.grad_ref, f32[1,128]{1,0:T(1,128)S(1)} %get-tuple-element.12.side_ref, f32[4,256]{1,0:T(4,128)S(1)} %copy-done.4), custom_call_target="tpu_custom_call" | custom-call | tf_op jit(solution)/shard_map/newton/pallas_call | solution.py:422
  102.7 0.7 reshape.32.new_ref
  103.4 0.0 copy-done.1
  103.4 16.0 %margins.1 = f32[1,2048]{1,0:T(1,128)S(1)} custom-call(f32[8,128]{1,0:T(8,128)S(1)} %reshape.32.new_ref, bf16[2048,256]{1,0:T(8,128)(2,1)S(1)} %copy-done.1, s32[1,2048]{1,0:T(1,128)S(1)} %get-tuple-element.15.slot_ref, f32[1,2048]{1,0:T(1,128)S(1)} %get-tuple-element.16.fixed_ref), custom_call_target="tpu_custom_call" | custom-call | tf_op jit(solution)/shard_map/margins/pallas_call | solution.py:449
  119.4 0.6 copy.12
Async XLA Ops:
  0.6 73.6 %copy-start.4 = (f32[4,256]{1,0:T(4,128)S(1)}, f32[4,256]{1,0:T(4,128)}, u32[]{:S(2)}) copy-start(f32[4,256]{1,0:T(4,128)} %coef_ref.1) | copy-start | bytes 12292
  1.4 1.2 %copy-start = (bf16[2048,256]{1,0:T(8,128)(2,1)S(1)}, bf16[2048,256]{1,0:T(8,128)(2,1)}, u32[]{:S(2)}) copy-start(bf16[2048,256]{1,0:T(8,128)(2,1)} %z_ref.3) | copy-start | bytes 3145732
  2.6 0.8 copy-start.2
  3.5 0.8 copy-start.3
  4.3 0.7 copy-start.5
  5.0 0.7 copy-start.6
  5.7 0.7 copy-start.7
  6.4 97.0 %copy-start.1 = (bf16[2048,256]{1,0:T(8,128)(2,1)S(1)}, bf16[2048,256]{1,0:T(8,128)(2,1)}, u32[]{:S(2)}) copy-start(bf16[2048,256]{1,0:T(8,128)(2,1)} %z_ref.3) | copy-start | bytes 3145732

commit v2 on v1

v2 whole, which is shorter than its diff:
```python
import functools

import jax
import jax.numpy as jnp
from jax import lax
from jax.experimental import pallas as pl
from jax.experimental.pallas import tpu as pltpu
from jax.sharding import PartitionSpec as P

R = 256
CAP = 8
LAMBDA = 1.0

MESH = pl.DeviceIdType.MESH
F32 = jnp.float32
BF16 = jnp.bfloat16
NT = (((1,), (1,)), ((), ()))
TN = (((0,), (0,)), ((), ()))
MIB = 1 << 20


def iota(shape, axis):
    return lax.broadcasted_iota(jnp.int32, shape, axis)


def halves(x):
    high = x.astype(BF16)
    return high, (x - high.astype(F32)).astype(BF16)


def thirds(x):
    high, rest = x.astype(BF16), None
    rest = x - high.astype(F32)
    middle = rest.astype(BF16)
    return high, middle, (rest - middle.astype(F32)).astype(BF16)


def place(device):
    return (device // 4, lax.rem(device, 4))


def position():
    return lax.axis_index("dp") * 4 + lax.axis_index("mp")


def one_hot(condition):
    return jnp.where(condition, 1.0, 0.0).astype(BF16)


def each_other(body):
    def some(i, carry):
        for j in range(8):
            body(1 + 8 * i + j)
        return carry

    lax.fori_loop(0, 15, some, 0)
    for k in range(121, 128):
        body(k)


def chip_and_core(me):
    return me // 8 * 4 + lax.rem(me, 4), lax.rem(me // 4, 2)


def table_place(me):
    chip, core = chip_and_core(me)
    return core * 64 + chip


def block_copy(table, blocks, peer, sem, number):
    return pltpu.make_async_remote_copy(
        src_ref=table.at[blocks],
        dst_ref=table.at[blocks],
        send_sem=sem.at[number],
        recv_sem=sem.at[2 + number],
        device_id=peer,
        device_id_type=MESH,
    )


def send_block(table, block, me, sem):
    chip, core = chip_and_core(me)
    at = table_place(me)
    table[pl.ds(at, 1)] = block.astype(BF16).reshape(1, 8, 128)

    def some(i, carry):
        for j in range(9):
            other = lax.rem(chip + (1 + 9 * i + j), 64)
            peer = (other // 4 * 2 + core, lax.rem(other, 4))
            block_copy(table, pl.ds(at, 1), peer, sem, 0).start()
        return carry

    lax.fori_loop(0, 7, some, 0)


def swap_blocks(table, me, sem):
    waiting = block_copy(table, pl.ds(0, 63), place(me), sem, 0)
    waiting.wait_send()
    waiting.wait_recv()
    _, core = chip_and_core(me)
    sibling = (me // 8 * 2 + 1 - core, lax.rem(me, 4))
    block_copy(table, pl.ds(core * 64, 64), sibling, sem, 1).start()


def finish_swap(table, wide, me, sem):
    waiting = block_copy(table, pl.ds(0, 64), place(me), sem, 1)
    waiting.wait_send()
    waiting.wait_recv()
    wide[...] = table[...].astype(F32).reshape(1024, 128)


def row_products(wide, z_ref, slot_ref, out_ref):
    half = [wide[pl.ds(h, 512, stride=2), :].astype(BF16) for h in range(2)]
    coefs = jnp.concatenate(half, axis=1)
    for c in range(8):
        lanes = pl.ds(256 * c, 256)
        product = lax.dot_general(coefs, z_ref[lanes, :], NT, preferred_element_type=F32)
        chosen = iota((512, 256), 0) == slot_ref[:, lanes]
        out_ref[:, lanes] = jnp.sum(jnp.where(chosen, product, 0.0), axis=0, keepdims=True)


def dispatch_kernel(
    v_hbm, ids_hbm, w_hbm, member_hbm, label_hbm, z_hbm, slots_hbm, coef_hbm,
    hess_ref, grad_ref, side_sum_ref, slot_ref, fixed_ref,
    v_ref, ids_ref, w_ref, member_ref, label_ref, z_ref, slots_ref, coef_ref,
    onehot, ids2, part, fixed_part, fixed_recv, table, wide, target_ref, score_ref,
    send, recv, side_send, side_recv,
    load_sem, table_sem, fixed_sem, side_sem, rows_send_sem, rows_recv_sem,
):
    me = position()
    mine = lax.axis_index("mp")
    group, inner = me // 8, lax.rem(me, 8)

    loads = [
        pltpu.make_async_copy(source, target, load_sem.at[n])
        for n, (source, target) in enumerate((
            (member_hbm, member_ref), (slots_hbm, slots_ref), (coef_hbm, coef_ref),
            (ids_hbm, ids_ref), (w_hbm, w_ref), (label_hbm, label_ref), (v_hbm, v_ref),
            (z_hbm, z_ref),
        ))
    ]
    for load in loads:
        load.start()

    barrier = pltpu.get_barrier_semaphore()

    def greet(k):
        peer = lax.rem(me + k, 128)
        pl.semaphore_signal(barrier, inc=1, device_id=place(peer), device_id_type=MESH)

    each_other(greet)

    loads[0].wait()
    loads[1].wait()
    for c in range(8):
        lanes = pl.ds(256 * c, 256)
        onehot[:, lanes] = one_hot(iota((512, 256), 0) == member_ref[:, lanes])
    slots = slots_ref[...]
    sub = iota((8, 512), 0)
    owner = slots // 4
    owner_row = jnp.where(sub == 1, lax.rem(slots, 4), jnp.where(sub == 2, table_place(owner), 0))
    owner_row = jnp.where(sub == 0, owner, owner_row).astype(F32).astype(BF16)
    before = one_hot(iota((256, 256), 0) < iota((256, 256), 1))
    tally = jnp.concatenate([before, jnp.ones((256, 256), BF16)], axis=1)
    base = jnp.zeros((512, 256), F32)
    for c in range(8):
        lanes = pl.ds(256 * c, 256)
        hot = onehot[:, lanes]
        found = jnp.dot(owner_row, hot, preferred_element_type=F32)
        counted = jnp.dot(hot, tally, preferred_element_type=F32)
        rank = jnp.sum(hot.astype(F32) * (base + counted[:, :256]), axis=0, keepdims=True)
        base = base + counted[:, 256:]
        slot_ref[:, lanes] = (found[2:3] * 4.0 + found[1:2]).astype(jnp.int32)
        target = found[0:1] * 32.0 + found[1:2] * 8.0 + rank
        target_ref[:, lanes] = target.astype(jnp.int32)

    for load in loads[2:]:
        load.wait()
    for r in range(64):
        for k in range(2):
            ids2[k, r:r + 1, :] = ids_ref[k:k + 1, 128 * r:128 * r + 128]
    spread = [one_hot(iota((128, 256), 1) == 2 * iota((128, 256), 0) + k) for k in range(2)]
    part[...] = sum(
        jnp.dot(ids2[k].astype(F32).astype(BF16), spread[k], preferred_element_type=F32)
        for k in range(2)
    )
    w2 = jnp.concatenate(halves(w_ref[...]), axis=1)

    def margin_rows(r, carry):
        rows = v_ref[pl.ds(pl.multiple_of(r * 256, 256), 256), :]
        product = lax.dot_general(
            w2, jnp.concatenate([rows, rows], axis=1), NT, preferred_element_type=F32
        )
        chosen = iota((128, 256), 0) == part[pl.ds(r, 1), :].astype(jnp.int32)
        part[pl.ds(r, 1), :] = jnp.sum(jnp.where(chosen, product, 0.0), axis=0, keepdims=True)
        return carry

    lax.fori_loop(0, 64, margin_rows, 0, unroll=4)
    pairs = one_hot(iota((256, 128), 0) // 2 == iota((256, 128), 1))
    fixed_part[...] = sum(
        jnp.dot(piece, pairs, preferred_element_type=F32) for piece in thirds(part[...])
    )

    pl.semaphore_wait(barrier, 127)
    for k in range(1, 4):
        other = lax.rem(mine + k, 4)
        pltpu.make_async_remote_copy(
            src_ref=fixed_part.at[pl.ds(pl.multiple_of(other * 16, 16), 16)],
            dst_ref=fixed_recv.at[pl.ds(k * 16, 16)],
            send_sem=fixed_sem.at[0],
            recv_sem=fixed_sem.at[1],
            device_id=(lax.axis_index("dp"), other),
            device_id_type=MESH,
        ).start()
    send_block(table, coef_ref[...], me, table_sem)

    def send_rows(phase, c):
        chunk = lax.rem(group + c, 16)
        target = target_ref[...] - chunk * 256
        picked = jnp.zeros((256, 256), F32)
        for piece in range(4):
            lanes = pl.ds(512 * piece, 512)
            hot = one_hot(iota((256, 512), 0) == target[:, 512 * piece:512 * piece + 512])
            picked = picked + jnp.dot(hot, z_ref[lanes, :], preferred_element_type=F32)
        send[pl.ds(chunk * 8, 8)] = picked.astype(BF16).reshape(8, 32, 256)

        def send_one(j):
            to = lax.rem(inner + j, 8)
            pltpu.make_async_remote_copy(
                src_ref=send.at[chunk * 8 + to],
                dst_ref=recv.at[me],
                send_sem=rows_send_sem,
                recv_sem=rows_recv_sem.at[phase],
                device_id=(chunk * 2 + to // 4, lax.rem(to, 4)),
                device_id_type=MESH,
            ).start()

        for j in range(1, 8):
            send_one(j)
        if isinstance(c, int) and c == 0:
            recv[pl.ds(me, 1)] = send[pl.ds(me, 1)]
        else:
            send_one(0)

    def send_phase(phase):
        def step(c, carry):
            send_rows(phase, c)
            return carry

        if phase == 0:
            send_rows(0, 0)
        lax.fori_loop(4 * phase + (phase == 0), 4 * phase + 4, step, 0)

    send_phase(0)
    send_phase(1)

    waiting = pltpu.make_async_remote_copy(
        src_ref=fixed_part.at[pl.ds(0, 48)],
        dst_ref=fixed_recv.at[pl.ds(16, 48)],
        send_sem=fixed_sem.at[0],
        recv_sem=fixed_sem.at[1],
        device_id=place(me),
        device_id_type=MESH,
    )
    waiting.wait_send()
    waiting.wait_recv()
    own = fixed_part[pl.ds(pl.multiple_of(mine * 16, 16), 16), :]
    total = own + fixed_recv[16:32] + fixed_recv[32:48] + fixed_recv[48:64]
    for r in range(16):
        fixed_ref[:, 128 * r:128 * r + 128] = total[r:r + 1, :]
    swap_blocks(table, me, table_sem)

    send_phase(2)

    finish_swap(table, wide, me, table_sem)
    row_products(wide, z_ref, slot_ref, score_ref)
    score = score_ref[...] + fixed_ref[...]
    label = label_ref[...].astype(F32)
    small = jnp.exp(-jnp.abs(score))
    probability = jnp.where(score >= 0.0, 1.0, small) / (1.0 + small)
    weight = small / ((1.0 + small) * (1.0 + small))
    residual = label - probability
    likelihood = label * score - (jnp.maximum(score, 0.0) + jnp.log1p(small))
    target = target_ref[...]
    total_side = jnp.zeros((128, 128), F32)
    for c in range(4):
        lanes = slice(512 * c, 512 * c + 512)
        owner_hot = one_hot(iota((128, 512), 0) == target[:, lanes] // 32)
        within = iota((32, 512), 0) == lax.rem(target[:, lanes], 32)
        sides = jnp.concatenate(
            [jnp.where(within, q[:, lanes], 0.0) for q in (weight, residual, likelihood)]
            + [jnp.zeros((32, 512), F32)],
            axis=0,
        )
        for piece in halves(sides):
            total_side = total_side + lax.dot_general(
                owner_hot, piece, NT, preferred_element_type=F32
            )
    for d in range(128):
        side_send[d] = total_side[d:d + 1, :]

    def side_copy(sources, targets, owner):
        return pltpu.make_async_remote_copy(
            src_ref=sources,
            dst_ref=targets,
            send_sem=side_sem.at[0],
            recv_sem=side_sem.at[1],
            device_id=place(owner),
            device_id_type=MESH,
        )

    def send_side(k):
        owner = lax.rem(me + k, 128)
        side_copy(side_send.at[owner], side_recv.at[me], owner).start()

    each_other(send_side)
    side_recv[pl.ds(me, 1)] = side_send[pl.ds(me, 1)]

    send_phase(3)

    waiting = side_copy(side_send.at[pl.ds(0, 127)], side_recv.at[pl.ds(0, 127)], me)
    waiting.wait_send()
    waiting.wait_recv()

    side_sum_ref[...] = jnp.sum(side_recv[...], axis=0)
    eye = jnp.where(iota((256, 256), 0) == iota((256, 256), 1), LAMBDA, 0.0)
    ones = jnp.ones((256, 128), BF16)
    lane = iota((32, 8, 128), 2) - iota((32, 8, 128), 1)
    for phase in range(4):
        count = 31 if phase == 0 else 32
        waiting = pltpu.make_async_remote_copy(
            src_ref=send.at[pl.ds(0, count)],
            dst_ref=recv.at[pl.ds(0, count)],
            send_sem=rows_send_sem,
            recv_sem=rows_recv_sem.at[phase],
            device_id=place(me),
            device_id_type=MESH,
        )
        waiting.wait_recv()
        starts = [lax.rem(group + 16 - (4 * phase + j), 16) * 8 for j in range(4)]
        sides = jnp.concatenate([side_recv[pl.ds(at, 8)] for at in starts], axis=0)
        sides = jnp.broadcast_to(sides, (32, 8, 128))
        for m in range(4):
            rows = jnp.concatenate(
                [recv[pl.ds(at, 8), 8 * m:8 * m + 8, :].astype(F32) for at in starts], axis=0
            ).reshape(256, 256)
            rows_b = rows.astype(BF16)
            column = []
            for quantity in range(2):
                chosen = lane == 32 * quantity + 8 * m
                picked = jnp.where(chosen, sides, 0.0).reshape(256, 128)
                picked = jnp.concatenate(halves(picked), axis=1)
                column.append(jnp.dot(picked, ones, preferred_element_type=F32))
            weights = jnp.concatenate([column[0], column[0]], axis=1)
            weighted = (weights * rows).astype(BF16)
            update = lax.dot_general(weighted, rows_b, TN, preferred_element_type=F32)
            pull = lax.dot_general(
                column[1].astype(BF16), rows_b, TN, preferred_element_type=F32
            )[0:8]
            if phase == 0:
                hess_ref[m] = eye + update
                grad_ref[m] = pull
            else:
                hess_ref[m] += update
                grad_ref[m] += pull
    waiting = pltpu.make_async_remote_copy(
        src_ref=send.at[pl.ds(0, 127)],
        dst_ref=recv.at[pl.ds(0, 127)],
        send_sem=rows_send_sem,
        recv_sem=rows_recv_sem.at[0],
        device_id=place(me),
        device_id_type=MESH,
    )
    waiting.wait_send()


def dispatch(v, ids, fixed_coef, member, labels, z, slots, coef8):
    vmem = pl.BlockSpec(memory_space=pltpu.VMEM)
    operands = (v, ids, fixed_coef, member, labels, z, slots, coef8)
    return pl.pallas_call(
        dispatch_kernel,
        out_shape=(
            jax.ShapeDtypeStruct((4, 256, 256), F32),
            jax.ShapeDtypeStruct((4, 8, 256), F32),
            jax.ShapeDtypeStruct((1, 128), F32),
            jax.ShapeDtypeStruct((1, 2048), jnp.int32),
            jax.ShapeDtypeStruct((1, 2048), F32),
        ),
        in_specs=[pl.BlockSpec(memory_space=pl.ANY)] * 8,
        out_specs=(vmem,) * 5,
        scratch_shapes=[pltpu.VMEM(x.shape, x.dtype) for x in operands] + [
            pltpu.VMEM((512, 2048), BF16),
            pltpu.VMEM((2, 64, 128), jnp.int32),
            pltpu.VMEM((64, 256), F32),
            pltpu.VMEM((64, 128), F32),
            pltpu.VMEM((64, 128), F32),
            pltpu.VMEM((128, 8, 128), BF16),
            pltpu.VMEM((1024, 128), F32),
            pltpu.VMEM((1, 2048), jnp.int32),
            pltpu.VMEM((1, 2048), F32),
            pltpu.VMEM((128, 32, 256), BF16),
            pltpu.VMEM((128, 32, 256), BF16),
            pltpu.VMEM((128, 1, 128), F32),
            pltpu.VMEM((128, 1, 128), F32),
            pltpu.SemaphoreType.DMA((8,)),
            pltpu.SemaphoreType.DMA((4,)),
            pltpu.SemaphoreType.DMA((2,)),
            pltpu.SemaphoreType.DMA((2,)),
            pltpu.SemaphoreType.DMA,
            pltpu.SemaphoreType.DMA((4,)),
        ],
        compiler_params=pltpu.CompilerParams(
            collective_id=0, has_side_effects=True, vmem_limit_bytes=56 * MIB
        ),
        name="dispatch",
    )(*operands)


def six_left(x, axis=0):
    high, middle, low = thirds(x)
    return jnp.concatenate([high, high, middle, middle, high, low], axis=axis)


def six_right(x, axis=0):
    high, middle, low = thirds(x)
    return jnp.concatenate([high, middle, high, middle, low, high], axis=axis)


def dot6(left, right, dims):
    ((la,), (ra,)), _ = dims
    return lax.dot_general(
        six_left(left, la), six_right(right, ra), dims, preferred_element_type=F32
    )


def factor_packed(packed, pivots, first, between):
    lane = iota((32, 128), 1)
    group = lane // 32 * 32
    local = lane - group
    sub = iota((32, 128), 0)
    local1 = local[0:1]
    roots = jnp.zeros((32, 128), F32)
    for j in range(0, 32, 4):
        below = sub >= j + 4
        columns = [
            jnp.take_along_axis(packed, group + (j + a), axis=1, mode="promise_in_bounds")
            for a in range(4)
        ]
        p = {(a, b): columns[b][j + a:j + a + 1] for a in range(4) for b in range(a, 4)}
        inside = (local1 >= j) & (local1 < j + 4)
        rows = [
            jnp.where(inside, jnp.where(local1 == j + a, 1.0, 0.0), packed[j + a:j + a + 1])
            for a in range(4)
        ]
        change = jnp.zeros((32, 128), F32)
        for a in range(4):
            scale = 1.0 / p[a, a]
            for b in range(a + 1, 4):
                ratio = p[a, b] * scale
                for c in range(b, 4):
                    p[b, c] = p[b, c] - ratio * p[a, c]
                rows[b] = rows[b] - ratio * rows[a]
                columns[b] = columns[b] - columns[a] * ratio
            change = change + columns[a] * (rows[a] * scale)
            pivots[first + j + a:first + j + a + 1, :] = p[a, a]
        kept = jnp.where((local >= j) & (local < j + 4), 0.0, packed) - change
        packed = jnp.where(below, kept, packed)
        for a in range(4):
            packed = jnp.where(sub == j + a, rows[a], packed)
            roots = jnp.where(sub == j + a, lax.rsqrt(p[a, a]), roots)
        between()
    return jnp.where(local <= sub, packed, 0.0) * roots


def solve_kernel(hess_ref, grad_ref, side_ref, coef_ref, new_ref, objective_ref, a_ref, pivots):
    lane = iota((1, 256), 1)
    for m in range(4):
        one_sided = hess_ref[m]
        a_ref[m] = 0.5 * (one_sided + one_sided.T)
    blocks = [a_ref[m, 0:32, :] for m in range(4)]
    pending = []

    def between():
        if pending:
            pending.pop(0)()

    for k in range(8):
        low = 32 * k
        packed = jnp.concatenate([b[:, low:low + 32] for b in blocks], axis=1)
        inverse = factor_packed(packed, pivots, low, between)
        while pending:
            between()
        inside = (lane >= low) & (lane < low + 32)
        sign = jnp.where(lane < low, -1.0, 1.0)
        following = []
        for m in range(4):
            own = inverse[:, 32 * m:32 * m + 32]
            wide = jnp.concatenate(
                ([jnp.zeros((32, low), F32)] if low else []) + [own]
                + ([jnp.zeros((32, 224 - low), F32)] if low < 224 else []),
                axis=1,
            )
            half = jnp.where(inside, wide, dot6(own, blocks[m], (((1,), (0,)), ((), ()))))
            left = six_left(half * sign)
            right = six_right(half)
            skipped = [k]
            if k < 7:
                change = lax.dot_general(
                    left[:, low + 32:low + 64], right, TN, preferred_element_type=F32
                )
                ahead = jnp.where(inside, 0.0, a_ref[m, low + 32:low + 64, :]) - change
                following.append(ahead)
                a_ref[m, low + 32:low + 64, :] = ahead
                skipped.append(k + 1)

            def bulk(part, m=m, low=low, own=own, left=left, right=right, inside=inside,
                     skipped=skipped):
                change = lax.dot_general(
                    left[:, 128 * part:128 * part + 128], right, TN, preferred_element_type=F32
                )
                for n in range(4):
                    if 4 * part + n not in skipped:
                        rows = slice(128 * part + 32 * n, 128 * part + 32 * n + 32)
                        a_ref[m, rows, :] = (
                            jnp.where(inside, 0.0, a_ref[m, rows, :]) - change[32 * n:32 * n + 32]
                        )
                if part == 1:
                    a_ref[m, low:low + 32, :] = lax.dot_general(
                        six_left(own), right, TN, preferred_element_type=F32
                    )

            pending += [functools.partial(bulk, part) for part in range(2)]
        blocks = following
    while pending:
        between()
    logs = jnp.sum(jnp.log(pivots[...]), axis=0, keepdims=True)
    side_lane = iota((1, 128), 1)
    for m in range(4):
        coef = coef_ref[m:m + 1, :]
        gradient = grad_ref[m] - LAMBDA * coef
        update = dot6(gradient, a_ref[m], (((1,), (0,)), ((), ())))
        new_ref[m:m + 1, :] = coef + update[0:1]
        half_logdet = 0.5 * jnp.sum(jnp.where(side_lane == 32 * m, logs, 0.0))
        mine = (side_lane >= 64 + 8 * m) & (side_lane < 72 + 8 * m)
        likelihood = jnp.sum(jnp.where(mine, side_ref[...], 0.0))
        objective_ref[m] = likelihood - 0.5 * LAMBDA * jnp.sum(coef * coef) - half_logdet


def solve(hess, grad, side_sum, coef):
    vmem = pl.BlockSpec(memory_space=pltpu.VMEM)
    return pl.pallas_call(
        solve_kernel,
        out_shape=(jax.ShapeDtypeStruct((4, 256), F32), jax.ShapeDtypeStruct((4,), F32)),
        in_specs=[vmem] * 4,
        out_specs=(vmem, pl.BlockSpec(memory_space=pltpu.SMEM)),
        scratch_shapes=[pltpu.VMEM((4, 256, 256), F32), pltpu.VMEM((256, 128), F32)],
        compiler_params=pltpu.CompilerParams(vmem_limit_bytes=32 * MIB),
        name="newton",
    )(hess, grad, side_sum, coef)


def margin_kernel(new_ref, z_ref, slot_ref, fixed_ref, out_ref, table, wide, sem):
    me = position()
    chip, core = chip_and_core(me)
    barrier = pltpu.get_barrier_semaphore()

    def greet(i, carry):
        for j in range(9):
            other = lax.rem(chip + (1 + 9 * i + j), 64)
            peer = (other // 4 * 2 + core, lax.rem(other, 4))
            pl.semaphore_signal(barrier, inc=1, device_id=peer, device_id_type=MESH)
        return carry

    lax.fori_loop(0, 7, greet, 0)
    sibling = (me // 8 * 2 + 1 - core, lax.rem(me, 4))
    pl.semaphore_signal(barrier, inc=1, device_id=sibling, device_id_type=MESH)
    pl.semaphore_wait(barrier, 64)
    send_block(table, new_ref[...], me, sem)
    swap_blocks(table, me, sem)
    finish_swap(table, wide, me, sem)
    row_products(wide, z_ref, slot_ref, out_ref)
    out_ref[...] += fixed_ref[...]


def margins(new8, z, slot, fixed):
    vmem = pl.BlockSpec(memory_space=pltpu.VMEM)
    return pl.pallas_call(
        margin_kernel,
        out_shape=jax.ShapeDtypeStruct((1, 2048), F32),
        in_specs=[vmem] * 4,
        out_specs=vmem,
        scratch_shapes=[
            pltpu.VMEM((128, 8, 128), BF16),
            pltpu.VMEM((1024, 128), F32),
            pltpu.SemaphoreType.DMA((4,)),
        ],
        compiler_params=pltpu.CompilerParams(
            collective_id=1, has_side_effects=True, vmem_limit_bytes=32 * MIB
        ),
        name="margins",
    )(new8, z, slot, fixed)


def shards(feat_values, feat_blocks, fixed_coef, member_of, labels, re_features, member_slot, coef):
    hess, grad, side_sum, slot, fixed = dispatch(
        feat_values.reshape(16384, 128),
        feat_blocks.T,
        fixed_coef,
        member_of.reshape(1, 2048),
        labels.reshape(1, 2048),
        re_features,
        member_slot.reshape(1, 512),
        coef.reshape(8, 128),
    )
    new_coef, objective = solve(hess, grad, side_sum, coef)
    margin = margins(new_coef.reshape(8, 128), re_features, slot, fixed)
    return (new_coef, objective, margin.reshape(2048))


def solution(mesh):
    placed = (
        P("dp", "mp", None),
        P("dp", "mp"),
        P(),
        P(("dp", "mp"), None),
        P(("dp", "mp")),
        P(("dp", "mp"), None),
        P(),
        P(("dp", "mp"), None),
    )
    return jax.shard_map(
        shards,
        mesh=mesh,
        in_specs=placed,
        out_specs=(P(("dp", "mp"), None), P(("dp", "mp")), P(("dp", "mp"))),
        check_vma=False,
    )
```

time: 122 us -> 94.8 us (0.78); the launches traced: 120 us -> 94.4 us
  Pallas kernels: 112 us -> 87 us
    pallas_call x1, Pallas kernels: 28.5 us -> 15 us  [solve(): pl.pallas_call(solve_kernel, out_shape=(jax.ShapeDtypeStruct((4, 256), F3...]
    pallas_call x1, Pallas kernels: 67.8 us -> 57.1 us  [dispatch(): pl.pallas_call(dispatch_kernel, out_shape=(jax.ShapeDtypeStruct((4, 256,...]
    unnamed x17 -> x15, local copies, waits for them, and re-layouts: 5.58 us -> 4.65 us
where the time goes in v2:
time: 94.8 us; the launch traced here: 94.4 us
  Pallas kernels  87 us (92%)
  local copies, waits for them, and re-layouts  6.72 us (7%)
    pallas_call x1, Pallas kernels, dispatch(): pl.pallas_call(dispatch_kernel, out_shape=(jax.ShapeDtypeStruct((4, 256,...  57.1 us
    pallas_call x1, Pallas kernels, solve(): pl.pallas_call(solve_kernel, out_shape=(jax.ShapeDtypeStruct((4, 256), F3...  15 us
    pallas_call x1, Pallas kernels, margins(): pl.pallas_call(margin_kernel, out_shape=jax.ShapeDtypeStruct((1, 2048), F...  14.9 us
    unnamed x15, local copies, waits for them, and re-layouts  4.65 us

profile of v2, /device:TPU:1, one launch (start us, length us, event | category | flops | bytes accessed | tf_op | source)
XLA Modules:
  0.0 94.4 jit_solution(12168384012791275948)
XLA Ops:
  0.6 0.0 copy-start.3
  0.6 0.0 copy-start
  0.7 1.4 %reshape.31.coef_hbm = f32[8,128]{1,0:T(8,128)} reshape(f32[4,256]{1,0:T(4,128)} %coef_ref.1) | data formatting | bytes 8192 | tf_op jit(solution)/shard_map/reshape | solution.py:613
  2.0 57.1 %dispatch.1 = (f32[4,256,256]{2,1,0:T(8,128)}, f32[4,8,256]{2,1,0:T(8,128)}, f32[1,128]{1,0:T(1,128)}, s32[1,2048]{1,0:T(1,128)}, f32[1,2048]{1,0:T(1,128)}) custom-call(bf16[16384,128]{1,0:T(8,128)(2,1)} %bitcast.7, s32[2,8192]{1,0:T(2,128)} %bitcast.8, f32[128,128]{1,0:T(8,128)} %w_hbm.1, s32[1,2048]{1,0:T(1,128)} %bitcast.9, s32[1,2048]{1,0:T(1,128)} %bitcast.10, ...), custom_call_target="tpu_custom_call" | custom-call | tf_op jit(solution)/shard_map/dispatch/pallas_call | solution.py:380
  59.1 0.0 copy-done.3
  59.1 0.0 copy-start.1
  59.1 1.2 %copy-done.1 = f32[4,256,256]{2,1,0:T(8,128)S(1)} copy-done((f32[4,256,256]{2,1,0:T(8,128)S(1)}, f32[4,256,256]{2,1,0:T(8,128)}, u32[]{:S(2)}) %copy-start.1) | copy-done | bytes 1048600
  60.4 0.0 copy-start.2
  60.4 0.8 copy-done.2
  61.1 0.0 copy-start.6
  61.1 0.7 copy-done.6
  61.8 15.0 %newton.1 = (f32[4,256]{1,0:T(4,128)}, f32[4]{0:T(128)}) custom-call(f32[4,256,256]{2,1,0:T(8,128)S(1)} %copy-done.1, f32[4,8,256]{2,1,0:T(8,128)S(1)} %copy-done.2, f32[1,128]{1,0:T(1,128)S(1)} %copy-done.6, f32[4,256]{1,0:T(4,128)S(1)} %copy-done.3), custom_call_target="tpu_custom_call" | custom-call | tf_op jit(solution)/shard_map/newton/pallas_call | solution.py:551
  76.8 0.7 reshape.32.new_ref
  77.5 0.0 copy-done
  77.5 0.0 copy-start.4
  77.5 0.7 copy-done.4
  78.2 0.0 copy-start.5
  78.2 0.7 copy-done.5
  78.9 14.9 %margins.1 = f32[1,2048]{1,0:T(1,128)S(1)} custom-call(f32[8,128]{1,0:T(8,128)S(1)} %reshape.32.new_ref, bf16[2048,256]{1,0:T(8,128)(2,1)S(1)} %copy-done, s32[1,2048]{1,0:T(1,128)S(1)} %copy-done.4, f32[1,2048]{1,0:T(1,128)S(1)} %copy-done.5), custom_call_target="tpu_custom_call" | custom-call | tf_op jit(solution)/shard_map/margins/pallas_call | solution.py:587
  93.8 0.6 copy.12
Async XLA Ops:
  0.6 58.5 %copy-start.3 = (f32[4,256]{1,0:T(4,128)S(1)}, f32[4,256]{1,0:T(4,128)}, u32[]{:S(2)}) copy-start(f32[4,256]{1,0:T(4,128)} %coef_ref.1) | copy-start | bytes 12292
  0.6 76.9 %copy-start = (bf16[2048,256]{1,0:T(8,128)(2,1)S(1)}, bf16[2048,256]{1,0:T(8,128)(2,1)}, u32[]{:S(2)}) copy-start(bf16[2048,256]{1,0:T(8,128)(2,1)} %z_ref.1) | copy-start | bytes 3145732
  59.1 1.2 %copy-start.1 = (f32[4,256,256]{2,1,0:T(8,128)S(1)}, f32[4,256,256]{2,1,0:T(8,128)}, u32[]{:S(2)}) copy-start(f32[4,256,256]{2,1,0:T(8,128)} %get-tuple-element.10.hess_ref) | copy-start | bytes 3145732
  60.4 0.8 copy-start.2
  61.1 0.7 copy-start.6
  77.5 0.7 copy-start.4
  78.2 0.7 copy-start.5

commit v3 on v0

v3 whole, which is shorter than its diff:
```python
import functools

import jax
import jax.numpy as jnp
from jax import lax
from jax.experimental import pallas as pl
from jax.experimental.pallas import tpu as pltpu
from jax.sharding import PartitionSpec as P

R = 256
CAP = 8
LAMBDA = 1.0

MESH = pl.DeviceIdType.MESH
F32 = jnp.float32
BF16 = jnp.bfloat16
NT = (((1,), (1,)), ((), ()))
TN = (((0,), (0,)), ((), ()))
MIB = 1 << 20


def iota(shape, axis):
    return lax.broadcasted_iota(jnp.int32, shape, axis)


def halves(x):
    high = x.astype(BF16)
    return high, (x - high.astype(F32)).astype(BF16)


def thirds(x):
    high, rest = x.astype(BF16), None
    rest = x - high.astype(F32)
    middle = rest.astype(BF16)
    return high, middle, (rest - middle.astype(F32)).astype(BF16)


def one_hot(condition):
    return jnp.where(condition, 1.0, 0.0).astype(BF16)


class Torus:
    def __init__(self):
        dp, self.y = lax.axis_index("dp"), lax.axis_index("mp")
        self.z, self.x, self.core = dp // 8, lax.rem(dp // 2, 4), lax.rem(dp, 2)
        self.zs = [lax.rem(self.z + d, 4) * 8 for d in range(4)]
        self.xs = [lax.rem(self.x + d, 4) * 2 for d in range(4)]
        self.cores = [self.core, 1 - self.core]
        self.ys = [lax.rem(self.y + d, 4) for d in range(4)]

    def peer(self, k):
        digits = 77 * k % 128
        dp = self.zs[digits // 32] + self.xs[digits // 8 % 4] + self.cores[digits // 4 % 2]
        return dp, self.ys[digits % 4]

    def step_of(self, owner):
        dz = lax.rem(owner // 32 + (4 - self.z), 4)
        dx = lax.rem(lax.rem(owner // 8, 4) + (4 - self.x), 4)
        core = lax.rem(lax.rem(owner // 4, 2) + (2 - self.core), 2)
        dy = lax.rem(lax.rem(owner, 4) + (4 - self.y), 4)
        return lax.rem(5 * (dz * 32 + dx * 8 + core * 4 + dy), 128)

    def chip_peer(self, k):
        digits = 29 * k % 64
        dp = self.zs[digits // 16] + self.xs[digits // 4 % 4] + self.core
        return dp, self.ys[digits % 4]

    def sibling(self):
        return self.zs[0] + self.xs[0] + self.cores[1], self.y

    def table_place(self):
        return self.core * 64 + self.z * 16 + self.x * 4 + self.y


def table_place(device):
    return lax.rem(device // 4, 2) * 64 + device // 8 * 4 + lax.rem(device, 4)


def remote(source, target, send_sem, recv_sem, peer):
    return pltpu.make_async_remote_copy(
        src_ref=source,
        dst_ref=target,
        send_sem=send_sem,
        recv_sem=recv_sem,
        device_id=peer,
        device_id_type=MESH,
    )


def row_products(wide, z_ref, slot_ref, out_ref):
    half = [wide[pl.ds(h, 512, stride=2), :].astype(BF16) for h in range(2)]
    coefs = jnp.concatenate(half, axis=1)
    for c in range(8):
        lanes = pl.ds(256 * c, 256)
        product = lax.dot_general(coefs, z_ref[lanes, :], NT, preferred_element_type=F32)
        chosen = iota((512, 256), 0) == slot_ref[:, lanes]
        out_ref[:, lanes] = jnp.sum(jnp.where(chosen, product, 0.0), axis=0, keepdims=True)


def six_left(x, axis=0):
    high, middle, low = thirds(x)
    return jnp.concatenate([high, high, middle, middle, high, low], axis=axis)


def six_right(x, axis=0):
    high, middle, low = thirds(x)
    return jnp.concatenate([high, middle, high, middle, low, high], axis=axis)


def dot6(left, right, dims):
    ((la,), (ra,)), _ = dims
    return lax.dot_general(
        six_left(left, la), six_right(right, ra), dims, preferred_element_type=F32
    )


def factor_packed(packed, pivots, first, between):
    lane = iota((32, 128), 1)
    group = lane // 32 * 32
    local = lane - group
    sub = iota((32, 128), 0)
    local1 = local[0:1]
    roots = jnp.zeros((32, 128), F32)
    for j in range(0, 32, 4):
        below = sub >= j + 4
        columns = [
            jnp.take_along_axis(packed, group + (j + a), axis=1, mode="promise_in_bounds")
            for a in range(4)
        ]
        p = {(a, b): columns[b][j + a:j + a + 1] for a in range(4) for b in range(a, 4)}
        inside = (local1 >= j) & (local1 < j + 4)
        rows = [
            jnp.where(inside, jnp.where(local1 == j + a, 1.0, 0.0), packed[j + a:j + a + 1])
            for a in range(4)
        ]
        change = jnp.zeros((32, 128), F32)
        for a in range(4):
            scale = 1.0 / p[a, a]
            for b in range(a + 1, 4):
                ratio = p[a, b] * scale
                for c in range(b, 4):
                    p[b, c] = p[b, c] - ratio * p[a, c]
                rows[b] = rows[b] - ratio * rows[a]
                columns[b] = columns[b] - columns[a] * ratio
            change = change + columns[a] * (rows[a] * scale)
            pivots[first + j + a:first + j + a + 1, :] = p[a, a]
        kept = jnp.where((local >= j) & (local < j + 4), 0.0, packed) - change
        packed = jnp.where(below, kept, packed)
        for a in range(4):
            packed = jnp.where(sub == j + a, rows[a], packed)
            roots = jnp.where(sub == j + a, lax.rsqrt(p[a, a]), roots)
        between()
    return jnp.where(local <= sub, packed, 0.0) * roots


def newton(a_ref, grad_ref, likelihood_ref, coef_ref, new_ref, objective_ref, pivots):
    lane = iota((1, 256), 1)
    for m in range(4):
        one_sided = a_ref[m]
        a_ref[m] = 0.5 * (one_sided + one_sided.T)
    blocks = [a_ref[m, 0:32, :] for m in range(4)]
    pending = []

    def between():
        if pending:
            pending.pop(0)()

    for k in range(8):
        low = 32 * k
        packed = jnp.concatenate([b[:, low:low + 32] for b in blocks], axis=1)
        inverse = factor_packed(packed, pivots, low, between)
        while pending:
            between()
        inside = (lane >= low) & (lane < low + 32)
        sign = jnp.where(lane < low, -1.0, 1.0)
        following = []
        for m in range(4):
            own = inverse[:, 32 * m:32 * m + 32]
            wide = jnp.concatenate(
                ([jnp.zeros((32, low), F32)] if low else []) + [own]
                + ([jnp.zeros((32, 224 - low), F32)] if low < 224 else []),
                axis=1,
            )
            half = jnp.where(inside, wide, dot6(own, blocks[m], (((1,), (0,)), ((), ()))))
            left = six_left(half * sign)
            right = six_right(half)
            skipped = [k]
            if k < 7:
                change = lax.dot_general(
                    left[:, low + 32:low + 64], right, TN, preferred_element_type=F32
                )
                ahead = jnp.where(inside, 0.0, a_ref[m, low + 32:low + 64, :]) - change
                following.append(ahead)
                a_ref[m, low + 32:low + 64, :] = ahead
                skipped.append(k + 1)

            def bulk(part, m=m, low=low, own=own, left=left, right=right, inside=inside,
                     skipped=skipped):
                change = lax.dot_general(
                    left[:, 128 * part:128 * part + 128], right, TN, preferred_element_type=F32
                )
                for n in range(4):
                    if 4 * part + n not in skipped:
                        rows = slice(128 * part + 32 * n, 128 * part + 32 * n + 32)
                        a_ref[m, rows, :] = (
                            jnp.where(inside, 0.0, a_ref[m, rows, :]) - change[32 * n:32 * n + 32]
                        )
                if part == 1:
                    a_ref[m, low:low + 32, :] = lax.dot_general(
                        six_left(own), right, TN, preferred_element_type=F32
                    )

            pending += [functools.partial(bulk, part) for part in range(2)]
        blocks = following
    while pending:
        between()
    logs = jnp.sum(jnp.log(pivots[...]), axis=0, keepdims=True)
    side_lane = iota((1, 128), 1)
    news = []
    for m in range(4):
        coef = coef_ref[m:m + 1, :]
        gradient = grad_ref[m] - LAMBDA * coef
        update = dot6(gradient, a_ref[m], (((1,), (0,)), ((), ())))
        new = coef + update[0:1]
        new_ref[m:m + 1, :] = new
        news += [new[:, :128], new[:, 128:]]
        logs_here = jnp.where(side_lane == 32 * m, logs, 0.0)
        half_logdet = 0.5 * jnp.sum(logs_here, axis=1, keepdims=True)
        square = jnp.sum(coef * coef, axis=1, keepdims=True)
        objective_ref[m:m + 1, :] = (
            likelihood_ref[m:m + 1, :] - 0.5 * LAMBDA * square - half_logdet
        )
    return jnp.concatenate(news, axis=0)


def step_kernel(
    v_hbm, ids_hbm, w_hbm, member_hbm, label_hbm, z_hbm, slots_hbm, coef_hbm,
    new_ref, objective_ref, margin_ref,
    v_ref, ids_ref, w_ref, member_ref, label_ref, z_ref, slots_ref, coef_ref,
    onehot, ids2, part, fixed_part, fixed_recv, fixed_ref, table, wide, target_ref, slot_ref,
    send, recv, side_send, side_recv, a_ref, grad_ref, likelihood_ref, pivots,
    load_sem, table_sem, fixed_sem, side_sem, rows_send_sem, rows_recv_sem,
):
    torus = Torus()

    loads = [
        pltpu.make_async_copy(source, target, load_sem.at[n])
        for n, (source, target) in enumerate((
            (member_hbm, member_ref), (slots_hbm, slots_ref), (coef_hbm, coef_ref),
            (ids_hbm, ids_ref), (w_hbm, w_ref), (label_hbm, label_ref), (v_hbm, v_ref),
            (z_hbm, z_ref),
        ))
    ]
    for load in loads:
        load.start()

    barrier = pltpu.get_barrier_semaphore()
    greeted = iter(range(1, 128))

    def greet(count):
        for _ in range(count):
            k = next(greeted, None)
            if k is not None:
                pl.semaphore_signal(
                    barrier, inc=1, device_id=torus.peer(k), device_id_type=MESH
                )

    loads[0].wait()
    loads[1].wait()
    for c in range(8):
        lanes = pl.ds(256 * c, 256)
        onehot[:, lanes] = one_hot(iota((512, 256), 0) == member_ref[:, lanes])
        greet(8)
    slots = slots_ref[...]
    sub = iota((8, 512), 0)
    owner = slots // 4
    owner_row = jnp.where(sub == 1, lax.rem(slots, 4), jnp.where(sub == 2, table_place(owner), 0))
    owner_row = jnp.where(sub == 0, torus.step_of(owner), owner_row).astype(F32).astype(BF16)
    before = one_hot(iota((256, 256), 0) < iota((256, 256), 1))
    tally = jnp.concatenate([before, jnp.ones((256, 256), BF16)], axis=1)
    base = jnp.zeros((512, 256), F32)
    for c in range(8):
        lanes = pl.ds(256 * c, 256)
        hot = onehot[:, lanes]
        found = jnp.dot(owner_row, hot, preferred_element_type=F32)
        counted = jnp.dot(hot, tally, preferred_element_type=F32)
        rank = jnp.sum(hot.astype(F32) * (base + counted[:, :256]), axis=0, keepdims=True)
        base = base + counted[:, 256:]
        slot_ref[:, lanes] = (found[2:3] * 4.0 + found[1:2]).astype(jnp.int32)
        target = found[0:1] * 32.0 + found[1:2] * 8.0 + rank
        target_ref[:, lanes] = target.astype(jnp.int32)
        greet(8)

    for load in loads[2:]:
        load.wait()
    for r in range(64):
        for k in range(2):
            ids2[k, r:r + 1, :] = ids_ref[k:k + 1, 128 * r:128 * r + 128]
    spread = [one_hot(iota((128, 256), 1) == 2 * iota((128, 256), 0) + k) for k in range(2)]
    part[...] = sum(
        jnp.dot(ids2[k].astype(F32).astype(BF16), spread[k], preferred_element_type=F32)
        for k in range(2)
    )
    w2 = jnp.concatenate(halves(w_ref[...]), axis=1)

    def margin_rows(r, carry):
        rows = v_ref[pl.ds(pl.multiple_of(r * 256, 256), 256), :]
        product = lax.dot_general(
            w2, jnp.concatenate([rows, rows], axis=1), NT, preferred_element_type=F32
        )
        chosen = iota((128, 256), 0) == part[pl.ds(r, 1), :].astype(jnp.int32)
        part[pl.ds(r, 1), :] = jnp.sum(jnp.where(chosen, product, 0.0), axis=0, keepdims=True)
        return carry

    lax.fori_loop(0, 64, margin_rows, 0, unroll=4)
    pairs = one_hot(iota((256, 128), 0) // 2 == iota((256, 128), 1))
    fixed_part[...] = sum(
        jnp.dot(piece, pairs, preferred_element_type=F32) for piece in thirds(part[...])
    )

    def pick_rows(c, carry):
        target = target_ref[...] - c * 256
        picked = jnp.zeros((256, 256), F32)
        for piece in range(4):
            lanes = pl.ds(512 * piece, 512)
            hot = one_hot(iota((256, 512), 0) == target[:, 512 * piece:512 * piece + 512])
            picked = picked + jnp.dot(hot, z_ref[lanes, :], preferred_element_type=F32)
        send[pl.ds(c * 8, 8)] = picked.astype(BF16).reshape(8, 32, 256)
        return carry

    def row_copy(places, k, phase):
        return remote(
            send.at[places], recv.at[places], rows_send_sem, rows_recv_sem.at[phase],
            torus.peer(k),
        )

    def send_rows(phase):
        for k in range(max(32 * phase, 1), 32 * phase + 32):
            row_copy(k, k, phase).start()

    lax.fori_loop(0, 4, pick_rows, 0)
    pl.semaphore_wait(barrier, 127)
    for k in range(1, 4):
        remote(
            fixed_part.at[pl.ds(pl.multiple_of(torus.ys[k] * 16, 16), 16)],
            fixed_recv.at[pl.ds(k * 16, 16)],
            fixed_sem.at[0], fixed_sem.at[1],
            (lax.axis_index("dp"), torus.ys[k]),
        ).start()
    send_rows(0)
    lax.fori_loop(4, 8, pick_rows, 0)
    send_rows(1)
    recv[0] = send[0]

    waiting = remote(
        fixed_part.at[pl.ds(0, 48)], fixed_recv.at[pl.ds(16, 48)],
        fixed_sem.at[0], fixed_sem.at[1], torus.peer(0),
    )
    waiting.wait_send()
    waiting.wait_recv()
    own = fixed_part[pl.ds(pl.multiple_of(torus.y * 16, 16), 16), :]
    total = own + fixed_recv[16:32] + fixed_recv[32:48] + fixed_recv[48:64]
    for r in range(16):
        fixed_ref[:, 128 * r:128 * r + 128] = total[r:r + 1, :]
    fixed = fixed_ref[...]
    code = label_ref[...].astype(F32) + 1.0
    target = target_ref[...]
    sides = jnp.zeros((128, 128), F32)
    for c in range(4):
        lanes = slice(512 * c, 512 * c + 512)
        step_hot = one_hot(iota((128, 512), 0) == target[:, lanes] // 32)
        within = iota((32, 512), 0) == lax.rem(target[:, lanes], 32)
        values = jnp.concatenate(
            [jnp.where(within, q[:, lanes], 0.0) for q in (fixed, code)]
            + [jnp.zeros((64, 512), F32)],
            axis=0,
        )
        for piece in thirds(values):
            sides = sides + lax.dot_general(step_hot, piece, NT, preferred_element_type=F32)
    for k in range(128):
        side_send[k] = sides[k:k + 1, :]

    def side_copy(places, k):
        return remote(
            side_send.at[places], side_recv.at[places], side_sem.at[0], side_sem.at[1],
            torus.peer(k),
        )

    for k in range(1, 128):
        side_copy(k, k).start()
    side_recv[0] = side_send[0]

    for phase in (2, 3):
        lax.fori_loop(4 * phase, 4 * phase + 4, pick_rows, 0)
        send_rows(phase)

    waiting = side_copy(pl.ds(0, 127), 0)
    waiting.wait_send()
    waiting.wait_recv()
    eye = jnp.where(iota((256, 256), 0) == iota((256, 256), 1), LAMBDA, 0.0)
    ones = jnp.ones((256, 128), BF16)
    lane = iota((32, 8, 128), 2) - iota((32, 8, 128), 1)
    for phase in range(4):
        row_copy(pl.ds(0, 31 if phase == 0 else 32), 0, phase).wait_recv()
        here = slice(32 * phase, 32 * phase + 32)
        sides = jnp.broadcast_to(side_recv[here], (32, 8, 128))
        for m in range(4):
            rows = recv[here, 8 * m:8 * m + 8, :].astype(F32).reshape(256, 256)
            rows_b = rows.astype(BF16)
            coef_b = jnp.broadcast_to(coef_ref[m:m + 1, :], (128, 256)).astype(BF16)
            known = jnp.where(lane == 8 * m, sides, 0.0).reshape(256, 128)
            known = jnp.concatenate(halves(known), axis=1)
            score = lax.dot_general(rows_b, coef_b, NT, preferred_element_type=F32)
            score = score + jnp.dot(known, ones, preferred_element_type=F32)
            code = jnp.where(lane == 32 + 8 * m, sides, 0.0).reshape(256, 128)
            code = jnp.dot(code.astype(BF16), ones[:128], preferred_element_type=F32)
            live = code > 0.5
            label = code - 1.0
            small = jnp.exp(-jnp.abs(score))
            inverse = 1.0 / (1.0 + small)
            probability = jnp.where(score >= 0.0, 1.0, small) * inverse
            weight = jnp.where(live, small * inverse * inverse, 0.0)
            residual = jnp.where(live, label - probability, 0.0).astype(BF16)
            gain = label * score - (jnp.maximum(score, 0.0) + jnp.log1p(small))
            gain = jnp.sum(jnp.where(live, gain, 0.0), axis=0, keepdims=True)
            weighted = (jnp.concatenate([weight, weight], axis=1) * rows).astype(BF16)
            update = lax.dot_general(weighted, rows_b, TN, preferred_element_type=F32)
            pull = lax.dot_general(residual, rows_b, TN, preferred_element_type=F32)[0:8]
            if phase == 0:
                a_ref[m] = eye + update
                grad_ref[m] = pull
                likelihood_ref[m:m + 1, :] = gain
            else:
                a_ref[m] += update
                grad_ref[m] += pull
                likelihood_ref[m:m + 1, :] += gain

    block = newton(a_ref, grad_ref, likelihood_ref, coef_ref, new_ref, objective_ref, pivots)
    row_copy(pl.ds(0, 127), 0, 0).wait_send()

    at = torus.table_place()
    table[pl.ds(at, 1)] = block.astype(BF16).reshape(1, 8, 128)

    def table_copy(blocks, number, peer):
        return remote(
            table.at[blocks], table.at[blocks], table_sem.at[number], table_sem.at[2 + number],
            peer,
        )

    for k in range(1, 64):
        table_copy(pl.ds(at, 1), 0, torus.chip_peer(k)).start()
    waiting = table_copy(pl.ds(0, 63), 0, torus.sibling())
    waiting.wait_send()
    waiting.wait_recv()
    swap = table_copy(pl.ds(torus.core * 64, 64), 1, torus.sibling())
    swap.start()
    swap.wait_send()
    swap.wait_recv()
    wide[...] = table[...].astype(F32).reshape(1024, 128)
    row_products(wide, z_ref, slot_ref, margin_ref)
    margin_ref[...] += fixed_ref[...]


def step(v, ids, fixed_coef, member, labels, z, slots, coef):
    vmem = pl.BlockSpec(memory_space=pltpu.VMEM)
    operands = (v, ids, fixed_coef, member, labels, z, slots, coef)
    return pl.pallas_call(
        step_kernel,
        out_shape=(
            jax.ShapeDtypeStruct((4, 256), F32),
            jax.ShapeDtypeStruct((4, 128), F32),
            jax.ShapeDtypeStruct((1, 2048), F32),
        ),
        in_specs=[pl.BlockSpec(memory_space=pl.ANY)] * 8,
        out_specs=(vmem,) * 3,
        scratch_shapes=[pltpu.VMEM(x.shape, x.dtype) for x in operands] + [
            pltpu.VMEM((512, 2048), BF16),
            pltpu.VMEM((2, 64, 128), jnp.int32),
            pltpu.VMEM((64, 256), F32),
            pltpu.VMEM((64, 128), F32),
            pltpu.VMEM((64, 128), F32),
            pltpu.VMEM((1, 2048), F32),
            pltpu.VMEM((128, 8, 128), BF16),
            pltpu.VMEM((1024, 128), F32),
            pltpu.VMEM((1, 2048), jnp.int32),
            pltpu.VMEM((1, 2048), jnp.int32),
            pltpu.VMEM((128, 32, 256), BF16),
            pltpu.VMEM((128, 32, 256), BF16),
            pltpu.VMEM((128, 1, 128), F32),
            pltpu.VMEM((128, 1, 128), F32),
            pltpu.VMEM((4, 256, 256), F32),
            pltpu.VMEM((4, 8, 256), F32),
            pltpu.VMEM((4, 128), F32),
            pltpu.VMEM((256, 128), F32),
            pltpu.SemaphoreType.DMA((8,)),
            pltpu.SemaphoreType.DMA((4,)),
            pltpu.SemaphoreType.DMA((2,)),
            pltpu.SemaphoreType.DMA((2,)),
            pltpu.SemaphoreType.DMA,
            pltpu.SemaphoreType.DMA((4,)),
        ],
        compiler_params=pltpu.CompilerParams(
            collective_id=0, has_side_effects=True, vmem_limit_bytes=56 * MIB
        ),
        name="step",
    )(*operands)


def shards(feat_values, feat_blocks, fixed_coef, member_of, labels, re_features, member_slot, coef):
    new_coef, objective, margin = step(
        feat_values.reshape(16384, 128),
        feat_blocks.T,
        fixed_coef,
        member_of.reshape(1, 2048),
        labels.reshape(1, 2048),
        re_features,
        member_slot.reshape(1, 512),
        coef,
    )
    return (new_coef, objective[:, 0], margin.reshape(2048))


def solution(mesh):
    placed = (
        P("dp", "mp", None),
        P("dp", "mp"),
        P(),
        P(("dp", "mp"), None),
        P(("dp", "mp")),
        P(("dp", "mp"), None),
        P(),
        P(("dp", "mp"), None),
    )
    return jax.shard_map(
        shards,
        mesh=mesh,
        in_specs=placed,
        out_specs=(P(("dp", "mp"), None), P(("dp", "mp")), P(("dp", "mp"))),
        check_vma=False,
    )
```

time: 576 us -> 78.2 us (0.14); the launches traced: 567 us -> 77.9 us
  other arithmetic: 299 us -> 0 us
  local copies, waits for them, and re-layouts: 174 us -> 3.84 us
  Pallas kernels: 0 us -> 73.4 us
  waiting for transfers between devices: 28.4 us -> 0 us
  starting transfers between devices: 26.5 us -> 0 us
  matrix products: 22.5 us -> 0 us
  blocking collectives: 15 us -> 0 us
    another operation x19 -> x0, other arithmetic: 222 us -> none  [the longest x10 139 us: shards(): factor = jnp.linalg.cholesky(hessian)]
    gather x5 -> x0, local copies, waits for them, and re-layouts: 93.5 us -> none  [the longest x1 54.4 us: shards(): fixed_coef[feat_blocks]]
    pallas_call x0 -> x1, Pallas kernels: none -> 73.4 us  [step(): pl.pallas_call(step_kernel, out_shape=(jax.ShapeDtypeStruct((4, 256), F32...]
    reduce_sum x4 -> x0, other arithmetic: 63.2 us -> none  [the longest x1 62.3 us: shards(): jnp.sum(feat_values.astype(jnp.float32) * fixed_coef[feat_blocks], axis=(...]
    all_to_all x3 -> x0, waiting for transfers between devices: 28.4 us -> none  [the longest x1 28.4 us: shards(): lax.all_to_all(send_rows.astype(jnp.float32), ('dp', 'mp'), split_axis=0,...]
    all_to_all x3 -> x0, starting transfers between devices: 26.5 us -> none  [the longest x1 12.7 us: shards(): lax.all_to_all(send_side, ('dp', 'mp'), split_axis=0, concat_axis=0, tile...]
    unnamed x37 -> x2, local copies, waits for them, and re-layouts: 26.4 us -> 2.56 us
    scatter x3 -> x0, local copies, waits for them, and re-layouts: 20.2 us -> none  [the longest x1 11.3 us: shards(): jnp.zeros((members * CAP, R), jnp.bfloat16).at[target].set(re_features)]
  transfers between devices with their start and end apart: 3 -> 0, of which waited for: 1 -> 0; matrix products, arithmetic and copies ran while one was open for 6% -> 0% of each run, Pallas kernels for 0% -> 0%
where the time goes in v3:
time: 78.2 us; the launch traced here: 77.9 us
  Pallas kernels  73.4 us (94%)
  local copies, waits for them, and re-layouts  3.84 us (5%)
    pallas_call x1, Pallas kernels, step(): pl.pallas_call(step_kernel, out_shape=(jax.ShapeDtypeStruct((4, 256), F32...  73.4 us
    unnamed x2, local copies, waits for them, and re-layouts  2.56 us

profile of v3, /device:TPU:1, one launch (start us, length us, event | category | flops | bytes accessed | tf_op | source)
XLA Modules:
  0.0 77.9 jit_solution(18142637536106146977)
XLA Ops:
  0.6 73.4 %step.1 = (f32[4,256]{1,0:T(4,128)}, f32[4,128]{1,0:T(4,128)}, f32[1,2048]{1,0:T(1,128)}) custom-call(bf16[16384,128]{1,0:T(8,128)(2,1)} %bitcast.6, s32[2,8192]{1,0:T(2,128)} %bitcast.7, f32[128,128]{1,0:T(8,128)} %w_hbm.1, s32[1,2048]{1,0:T(1,128)} %bitcast.8, s32[1,2048]{1,0:T(1,128)} %bitcast.9, bf16[2048,256]{1,0:T(8,128)(2,1)} %z_hbm.1, ...), custom_call_target="tpu_custom_call" | custom-call | tf_op jit(solution)/shard_map/step/pallas_call | solution.py:467
  74.0 1.3 %slice_reduce_fusion = f32[4]{0:T(128)} fusion(f32[4,128]{1,0:T(4,128)} %get-tuple-element.7), kind=kLoop, calls=%fused_computation | loop fusion | bytes 32 | tf_op jit(solution)/shard_map/slice | solution.py:520
  75.3 1.3 %copy.13 = f32[4,256]{1,0:T(4,128)} copy(f32[4,256]{1,0:T(4,128)} %get-tuple-element.12) | data formatting | bytes 8192
  76.6 1.3 %copy.14 = f32[2048]{0:T(1024)} copy(f32[2048]{0:T(1024)} %bitcast.10) | data formatting | bytes 16384

commit v4 on v3

--- a/solution.py
+++ b/solution.py
@@ -17,6 +17,7 @@
 NT = (((1,), (1,)), ((), ()))
 TN = (((0,), (0,)), ((), ()))
 MIB = 1 << 20
+PHASES = (0, 40, 80, 112, 128)
 
 
 def iota(shape, axis):
@@ -121,34 +122,35 @@
     sub = iota((32, 128), 0)
     local1 = local[0:1]
     roots = jnp.zeros((32, 128), F32)
-    for j in range(0, 32, 4):
-        below = sub >= j + 4
+    for j in range(0, 32, 8):
+        below = sub >= j + 8
         columns = [
             jnp.take_along_axis(packed, group + (j + a), axis=1, mode="promise_in_bounds")
-            for a in range(4)
+            for a in range(8)
         ]
-        p = {(a, b): columns[b][j + a:j + a + 1] for a in range(4) for b in range(a, 4)}
-        inside = (local1 >= j) & (local1 < j + 4)
+        p = {(a, b): columns[b][j + a:j + a + 1] for a in range(8) for b in range(a, 8)}
+        inside = (local1 >= j) & (local1 < j + 8)
         rows = [
             jnp.where(inside, jnp.where(local1 == j + a, 1.0, 0.0), packed[j + a:j + a + 1])
-            for a in range(4)
+            for a in range(8)
         ]
         change = jnp.zeros((32, 128), F32)
-        for a in range(4):
+        for a in range(8):
             scale = 1.0 / p[a, a]
-            for b in range(a + 1, 4):
+            for b in range(a + 1, 8):
                 ratio = p[a, b] * scale
-                for c in range(b, 4):
+                for c in range(b, 8):
                     p[b, c] = p[b, c] - ratio * p[a, c]
                 rows[b] = rows[b] - ratio * rows[a]
                 columns[b] = columns[b] - columns[a] * ratio
             change = change + columns[a] * (rows[a] * scale)
             pivots[first + j + a:first + j + a + 1, :] = p[a, a]
-        kept = jnp.where((local >= j) & (local < j + 4), 0.0, packed) - change
+        kept = jnp.where((local >= j) & (local < j + 8), 0.0, packed) - change
         packed = jnp.where(below, kept, packed)
-        for a in range(4):
+        for a in range(8):
             packed = jnp.where(sub == j + a, rows[a], packed)
             roots = jnp.where(sub == j + a, lax.rsqrt(p[a, a]), roots)
+        between()
         between()
     return jnp.where(local <= sub, packed, 0.0) * roots
 
@@ -224,12 +226,9 @@
         new = coef + update[0:1]
         new_ref[m:m + 1, :] = new
         news += [new[:, :128], new[:, 128:]]
-        logs_here = jnp.where(side_lane == 32 * m, logs, 0.0)
-        half_logdet = 0.5 * jnp.sum(logs_here, axis=1, keepdims=True)
-        square = jnp.sum(coef * coef, axis=1, keepdims=True)
-        objective_ref[m:m + 1, :] = (
-            likelihood_ref[m:m + 1, :] - 0.5 * LAMBDA * square - half_logdet
-        )
+        half_logdet = 0.5 * jnp.sum(jnp.where(side_lane == 32 * m, logs, 0.0))
+        likelihood = jnp.sum(jnp.where(side_lane == 0, likelihood_ref[m:m + 1, :], 0.0))
+        objective_ref[m] = likelihood - 0.5 * LAMBDA * jnp.sum(coef * coef) - half_logdet
     return jnp.concatenate(news, axis=0)
 
 
@@ -246,9 +245,9 @@
     loads = [
         pltpu.make_async_copy(source, target, load_sem.at[n])
         for n, (source, target) in enumerate((
-            (member_hbm, member_ref), (slots_hbm, slots_ref), (coef_hbm, coef_ref),
-            (ids_hbm, ids_ref), (w_hbm, w_ref), (label_hbm, label_ref), (v_hbm, v_ref),
-            (z_hbm, z_ref),
+            (member_hbm, member_ref), (slots_hbm, slots_ref), (z_hbm, z_ref),
+            (ids_hbm, ids_ref), (w_hbm, w_ref), (v_hbm, v_ref), (label_hbm, label_ref),
+            (coef_hbm, coef_ref),
         ))
     ]
     for load in loads:
@@ -265,12 +264,13 @@
                     barrier, inc=1, device_id=torus.peer(k), device_id_type=MESH
                 )
 
+    greet(47)
     loads[0].wait()
     loads[1].wait()
     for c in range(8):
         lanes = pl.ds(256 * c, 256)
         onehot[:, lanes] = one_hot(iota((512, 256), 0) == member_ref[:, lanes])
-        greet(8)
+        greet(5)
     slots = slots_ref[...]
     sub = iota((8, 512), 0)
     owner = slots // 4
@@ -289,34 +289,7 @@
         slot_ref[:, lanes] = (found[2:3] * 4.0 + found[1:2]).astype(jnp.int32)
         target = found[0:1] * 32.0 + found[1:2] * 8.0 + rank
         target_ref[:, lanes] = target.astype(jnp.int32)
-        greet(8)
-
-    for load in loads[2:]:
-        load.wait()
-    for r in range(64):
-        for k in range(2):
-            ids2[k, r:r + 1, :] = ids_ref[k:k + 1, 128 * r:128 * r + 128]
-    spread = [one_hot(iota((128, 256), 1) == 2 * iota((128, 256), 0) + k) for k in range(2)]
-    part[...] = sum(
-        jnp.dot(ids2[k].astype(F32).astype(BF16), spread[k], preferred_element_type=F32)
-        for k in range(2)
-    )
-    w2 = jnp.concatenate(halves(w_ref[...]), axis=1)
-
-    def margin_rows(r, carry):
-        rows = v_ref[pl.ds(pl.multiple_of(r * 256, 256), 256), :]
-        product = lax.dot_general(
-            w2, jnp.concatenate([rows, rows], axis=1), NT, preferred_element_type=F32
-        )
-        chosen = iota((128, 256), 0) == part[pl.ds(r, 1), :].astype(jnp.int32)
-        part[pl.ds(r, 1), :] = jnp.sum(jnp.where(chosen, product, 0.0), axis=0, keepdims=True)
-        return carry
-
-    lax.fori_loop(0, 64, margin_rows, 0, unroll=4)
-    pairs = one_hot(iota((256, 128), 0) // 2 == iota((256, 128), 1))
-    fixed_part[...] = sum(
-        jnp.dot(piece, pairs, preferred_element_type=F32) for piece in thirds(part[...])
-    )
+        greet(5)
 
     def pick_rows(c, carry):
         target = target_ref[...] - c * 256
@@ -334,11 +307,46 @@
             torus.peer(k),
         )
 
-    def send_rows(phase):
-        for k in range(max(32 * phase, 1), 32 * phase + 32):
+    def pick(low, high):
+        lax.fori_loop(low // 8, high // 8, pick_rows, 0)
+
+    def send_rows(low, high, phase):
+        for k in range(max(low, 1), high):
             row_copy(k, k, phase).start()
 
-    lax.fori_loop(0, 4, pick_rows, 0)
+    def send_phase(phase):
+        pick(PHASES[phase], PHASES[phase + 1])
+        send_rows(PHASES[phase], PHASES[phase + 1], phase)
+
+    for load in loads[3:]:
+        load.wait()
+    for r in range(64):
+        for k in range(2):
+            ids2[k, r:r + 1, :] = ids_ref[k:k + 1, 128 * r:128 * r + 128]
+    spread = [one_hot(iota((128, 256), 1) == 2 * iota((128, 256), 0) + k) for k in range(2)]
+    part[...] = sum(
+        jnp.dot(ids2[k].astype(F32).astype(BF16), spread[k], preferred_element_type=F32)
+        for k in range(2)
+    )
+    w2 = jnp.concatenate(halves(w_ref[...]), axis=1)
+
+    def margin_rows(r, carry):
+        rows = v_ref[pl.ds(pl.multiple_of(r * 256, 256), 256), :]
+        product = lax.dot_general(
+            w2, jnp.concatenate([rows, rows], axis=1), NT, preferred_element_type=F32
+        )
+        chosen = iota((128, 256), 0) == part[pl.ds(r, 1), :].astype(jnp.int32)
+        part[pl.ds(r, 1), :] = jnp.sum(jnp.where(chosen, product, 0.0), axis=0, keepdims=True)
+        return carry
+
+    lax.fori_loop(0, 64, margin_rows, 0, unroll=4)
+    pairs = one_hot(iota((256, 128), 0) // 2 == iota((256, 128), 1))
+    fixed_part[...] = sum(
+        jnp.dot(piece, pairs, preferred_element_type=F32) for piece in thirds(part[...])
+    )
+
+    loads[2].wait()
+    pick(0, 16)
     pl.semaphore_wait(barrier, 127)
     for k in range(1, 4):
         remote(
@@ -347,9 +355,9 @@
             fixed_sem.at[0], fixed_sem.at[1],
             (lax.axis_index("dp"), torus.ys[k]),
         ).start()
-    send_rows(0)
-    lax.fori_loop(4, 8, pick_rows, 0)
-    send_rows(1)
+    send_rows(0, 16, 0)
+    pick(16, PHASES[1])
+    send_rows(16, PHASES[1], 0)
     recv[0] = send[0]
 
     waiting = remote(
@@ -390,29 +398,29 @@
         side_copy(k, k).start()
     side_recv[0] = side_send[0]
 
-    for phase in (2, 3):
-        lax.fori_loop(4 * phase, 4 * phase + 4, pick_rows, 0)
-        send_rows(phase)
+    for phase in (1, 2, 3):
+        send_phase(phase)
 
     waiting = side_copy(pl.ds(0, 127), 0)
     waiting.wait_send()
     waiting.wait_recv()
     eye = jnp.where(iota((256, 256), 0) == iota((256, 256), 1), LAMBDA, 0.0)
     ones = jnp.ones((256, 128), BF16)
-    lane = iota((32, 8, 128), 2) - iota((32, 8, 128), 1)
     for phase in range(4):
-        row_copy(pl.ds(0, 31 if phase == 0 else 32), 0, phase).wait_recv()
-        here = slice(32 * phase, 32 * phase + 32)
-        sides = jnp.broadcast_to(side_recv[here], (32, 8, 128))
+        low, high = PHASES[phase], PHASES[phase + 1]
+        count = high - low
+        row_copy(pl.ds(0, count - (phase == 0)), 0, phase).wait_recv()
+        lane = iota((count, 8, 128), 2) - iota((count, 8, 128), 1)
+        sides = jnp.broadcast_to(side_recv[low:high], (count, 8, 128))
         for m in range(4):
-            rows = recv[here, 8 * m:8 * m + 8, :].astype(F32).reshape(256, 256)
+            rows = recv[low:high, 8 * m:8 * m + 8, :].astype(F32).reshape(8 * count, 256)
             rows_b = rows.astype(BF16)
             coef_b = jnp.broadcast_to(coef_ref[m:m + 1, :], (128, 256)).astype(BF16)
-            known = jnp.where(lane == 8 * m, sides, 0.0).reshape(256, 128)
+            known = jnp.where(lane == 8 * m, sides, 0.0).reshape(8 * count, 128)
             known = jnp.concatenate(halves(known), axis=1)
             score = lax.dot_general(rows_b, coef_b, NT, preferred_element_type=F32)
             score = score + jnp.dot(known, ones, preferred_element_type=F32)
-            code = jnp.where(lane == 32 + 8 * m, sides, 0.0).reshape(256, 128)
+            code = jnp.where(lane == 32 + 8 * m, sides, 0.0).reshape(8 * count, 128)
             code = jnp.dot(code.astype(BF16), ones[:128], preferred_element_type=F32)
             live = code > 0.5
             label = code - 1.0
@@ -468,11 +476,11 @@
         step_kernel,
         out_shape=(
             jax.ShapeDtypeStruct((4, 256), F32),
-            jax.ShapeDtypeStruct((4, 128), F32),
+            jax.ShapeDtypeStruct((4,), F32),
             jax.ShapeDtypeStruct((1, 2048), F32),
         ),
         in_specs=[pl.BlockSpec(memory_space=pl.ANY)] * 8,
-        out_specs=(vmem,) * 3,
+        out_specs=(vmem, pl.BlockSpec(memory_space=pltpu.SMEM), vmem),
         scratch_shapes=[pltpu.VMEM(x.shape, x.dtype) for x in operands] + [
             pltpu.VMEM((512, 2048), BF16),
             pltpu.VMEM((2, 64, 128), jnp.int32),
@@ -506,6 +514,29 @@
     )(*operands)
 
 
+def hand_over_kernel(*refs):
+    count = (len(refs) - 1) // 2
+    copies = [
+        pltpu.make_async_copy(refs[n], refs[count + n], refs[-1].at[n]) for n in range(count)
+    ]
+    for copy in copies:
+        copy.start()
+    for copy in copies:
+        copy.wait()
+
+
+def hand_over(*arrays):
+    anywhere = pl.BlockSpec(memory_space=pl.ANY)
+    return pl.pallas_call(
+        hand_over_kernel,
+        out_shape=tuple(jax.ShapeDtypeStruct(x.shape, x.dtype) for x in arrays),
+        in_specs=[anywhere] * len(arrays),
+        out_specs=(anywhere,) * len(arrays),
+        scratch_shapes=[pltpu.SemaphoreType.DMA((len(arrays),))],
+        name="hand_over",
+    )(*arrays)
+
+
 def shards(feat_values, feat_blocks, fixed_coef, member_of, labels, re_features, member_slot, coef):
     new_coef, objective, margin = step(
         feat_values.reshape(16384, 128),
@@ -517,7 +548,8 @@
         member_slot.reshape(1, 512),
         coef,
     )
-    return (new_coef, objective[:, 0], margin.reshape(2048))
+    new_coef, objective, margin = hand_over(new_coef, objective, margin)
+    return (new_coef, objective, margin.reshape(2048))
 
 
 def solution(mesh):

time: 78.2 us -> 72.3 us (0.925)
  local copies, waits for them, and re-layouts: 3.84 us -> 0 us
  Pallas kernels: 73.4 us -> 71.3 us
    pallas_call x1, Pallas kernels: 73.4 us -> 69.8 us  [step(): pl.pallas_call(step_kernel, out_shape=(jax.ShapeDtypeStruct((4, 256), F32...]
    unnamed x2 -> x0, local copies, waits for them, and re-layouts: 2.56 us -> none
    pallas_call x0 -> x1, Pallas kernels: none -> 1.52 us  [hand_over(): pl.pallas_call(hand_over_kernel, out_shape=tuple((jax.ShapeDtypeStruct(x....]
    slice x1 -> x0, local copies, waits for them, and re-layouts: 1.28 us -> none  [shards(): return (new_coef, objective[:, 0], margin.reshape(2048))]
where the time goes in v4:
time: 72.3 us; the launch traced here: 72.1 us
  Pallas kernels  71.3 us (99%)
  between operations  0.82 us (1%)
    pallas_call x1, Pallas kernels, step(): pl.pallas_call(step_kernel, out_shape=(jax.ShapeDtypeStruct((4, 256), F32...  69.8 us
    pallas_call x1, Pallas kernels, hand_over(): pl.pallas_call(hand_over_kernel, out_shape=tuple((jax.ShapeDtypeStruct(x....  1.52 us

profile of v4, /device:TPU:1, one launch (start us, length us, event | category | flops | bytes accessed | tf_op | source)
XLA Modules:
  0.0 72.1 jit_solution(12705824147909944498)
XLA Ops:
  0.6 69.8 %step.1 = (f32[4,256]{1,0:T(4,128)}, f32[4]{0:T(128)}, f32[1,2048]{1,0:T(1,128)}) custom-call(bf16[16384,128]{1,0:T(8,128)(2,1)} %bitcast.6, s32[2,8192]{1,0:T(2,128)} %bitcast.7, f32[128,128]{1,0:T(8,128)} %w_hbm.1, s32[1,2048]{1,0:T(1,128)} %bitcast.8, s32[1,2048]{1,0:T(1,128)} %bitcast.9, bf16[2048,256]{1,0:T(8,128)(2,1)} %z_hbm.1, s32[1,512]{1,0:T(1,128)} %bitcast.10, ...), custom_call_target="tpu_custom_call" | custom-call | tf_op jit(solution)/shard_map/step/pallas_call | solution.py:475
  70.4 1.5 %hand_over.1 = (f32[4,256]{1,0:T(4,128)}, f32[4]{0:T(128)}, f32[1,2048]{1,0:T(1,128)}) custom-call(f32[4,256]{1,0:T(4,128)} %get-tuple-element.9.refs_0_, f32[4]{0:T(128)} %get-tuple-element.10.refs_1_, f32[1,2048]{1,0:T(1,128)} %get-tuple-element.11.refs_2_), custom_call_target="tpu_custom_call" | custom-call | tf_op jit(solution)/shard_map/hand_over/pallas_call | solution.py:530

commit v5 on v4

--- a/solution.py
+++ b/solution.py
@@ -88,14 +88,14 @@
     )
 
 
-def row_products(wide, z_ref, slot_ref, out_ref):
-    half = [wide[pl.ds(h, 512, stride=2), :].astype(BF16) for h in range(2)]
+def add_row_products(wide, first, z_ref, slot_ref, out_ref):
+    half = [wide[pl.ds(first * 2 + h, 256, stride=2), :].astype(BF16) for h in range(2)]
     coefs = jnp.concatenate(half, axis=1)
     for c in range(8):
         lanes = pl.ds(256 * c, 256)
         product = lax.dot_general(coefs, z_ref[lanes, :], NT, preferred_element_type=F32)
-        chosen = iota((512, 256), 0) == slot_ref[:, lanes]
-        out_ref[:, lanes] = jnp.sum(jnp.where(chosen, product, 0.0), axis=0, keepdims=True)
+        chosen = iota((256, 256), 0) == slot_ref[:, lanes] - first
+        out_ref[:, lanes] += jnp.sum(jnp.where(chosen, product, 0.0), axis=0, keepdims=True)
 
 
 def six_left(x, axis=0):
@@ -264,7 +264,7 @@
                     barrier, inc=1, device_id=torus.peer(k), device_id_type=MESH
                 )
 
-    greet(47)
+    greet(127)
     loads[0].wait()
     loads[1].wait()
     for c in range(8):
@@ -398,7 +398,7 @@
         side_copy(k, k).start()
     side_recv[0] = side_send[0]
 
-    for phase in (1, 2, 3):
+    for phase in range(1, len(PHASES) - 1):
         send_phase(phase)
 
     waiting = side_copy(pl.ds(0, 127), 0)
@@ -406,7 +406,7 @@
     waiting.wait_recv()
     eye = jnp.where(iota((256, 256), 0) == iota((256, 256), 1), LAMBDA, 0.0)
     ones = jnp.ones((256, 128), BF16)
-    for phase in range(4):
+    for phase in range(len(PHASES) - 1):
         low, high = PHASES[phase], PHASES[phase + 1]
         count = high - low
         row_copy(pl.ds(0, count - (phase == 0)), 0, phase).wait_recv()
@@ -462,11 +462,18 @@
     waiting.wait_recv()
     swap = table_copy(pl.ds(torus.core * 64, 64), 1, torus.sibling())
     swap.start()
+    margin_ref[...] = fixed_ref[...]
+
+    def add_margins(core):
+        here = pl.ds(core * 64, 64)
+        rows = pl.ds(pl.multiple_of(core * 512, 512), 512)
+        wide[rows, :] = table[here].astype(F32).reshape(512, 128)
+        add_row_products(wide, core * 256, z_ref, slot_ref, margin_ref)
+
+    add_margins(torus.core)
     swap.wait_send()
     swap.wait_recv()
-    wide[...] = table[...].astype(F32).reshape(1024, 128)
-    row_products(wide, z_ref, slot_ref, margin_ref)
-    margin_ref[...] += fixed_ref[...]
+    add_margins(torus.cores[1])
 
 
 def step(v, ids, fixed_coef, member, labels, z, slots, coef):
@@ -505,7 +512,7 @@
             pltpu.SemaphoreType.DMA((2,)),
             pltpu.SemaphoreType.DMA((2,)),
             pltpu.SemaphoreType.DMA,
-            pltpu.SemaphoreType.DMA((4,)),
+            pltpu.SemaphoreType.DMA((len(PHASES) - 1,)),
         ],
         compiler_params=pltpu.CompilerParams(
             collective_id=0, has_side_effects=True, vmem_limit_bytes=56 * MIB

time: 72.3 us -> 70.1 us (0.970)
  Pallas kernels: 71.3 us -> 69.1 us
    pallas_call x1, Pallas kernels: 69.8 us -> 67.6 us  [step(): pl.pallas_call(step_kernel, out_shape=(jax.ShapeDtypeStruct((4, 256), F32...]
where the time goes in v5:
time: 70.1 us; the launch traced here: 70 us
  Pallas kernels  69.1 us (99%)
  between operations  0.82 us (1%)
    pallas_call x1, Pallas kernels, step(): pl.pallas_call(step_kernel, out_shape=(jax.ShapeDtypeStruct((4, 256), F32...  67.6 us
    pallas_call x1, Pallas kernels, hand_over(): pl.pallas_call(hand_over_kernel, out_shape=tuple((jax.ShapeDtypeStruct(x....  1.52 us

profile of v5, /device:TPU:1, one launch (start us, length us, event | category | flops | bytes accessed | tf_op | source)
XLA Modules:
  0.0 70.0 jit_solution(2672941706151116369)
XLA Ops:
  0.6 67.6 %step.1 = (f32[4,256]{1,0:T(4,128)}, f32[4]{0:T(128)}, f32[1,2048]{1,0:T(1,128)}) custom-call(bf16[16384,128]{1,0:T(8,128)(2,1)} %bitcast.6, s32[2,8192]{1,0:T(2,128)} %bitcast.7, f32[128,128]{1,0:T(8,128)} %w_hbm.1, s32[1,2048]{1,0:T(1,128)} %bitcast.8, s32[1,2048]{1,0:T(1,128)} %bitcast.9, bf16[2048,256]{1,0:T(8,128)(2,1)} %z_hbm.1, s32[1,512]{1,0:T(1,128)} %bitcast.10, ...), custom_call_target="tpu_custom_call" | custom-call | tf_op jit(solution)/shard_map/step/pallas_call | solution.py:482
  68.3 1.5 %hand_over.1 = (f32[4,256]{1,0:T(4,128)}, f32[4]{0:T(128)}, f32[1,2048]{1,0:T(1,128)}) custom-call(f32[4,256]{1,0:T(4,128)} %get-tuple-element.9.refs_0_, f32[4]{0:T(128)} %get-tuple-element.10.refs_1_, f32[1,2048]{1,0:T(1,128)} %get-tuple-element.11.refs_2_), custom_call_target="tpu_custom_call" | custom-call | tf_op jit(solution)/shard_map/hand_over/pallas_call | solution.py:537

commit v6 on v5

--- a/solution.py
+++ b/solution.py
@@ -339,14 +339,14 @@
         part[pl.ds(r, 1), :] = jnp.sum(jnp.where(chosen, product, 0.0), axis=0, keepdims=True)
         return carry
 
-    lax.fori_loop(0, 64, margin_rows, 0, unroll=4)
+    lax.fori_loop(0, 64, margin_rows, 0, unroll=8)
     pairs = one_hot(iota((256, 128), 0) // 2 == iota((256, 128), 1))
     fixed_part[...] = sum(
         jnp.dot(piece, pairs, preferred_element_type=F32) for piece in thirds(part[...])
     )
 
     loads[2].wait()
-    pick(0, 16)
+    pick(0, 8)
     pl.semaphore_wait(barrier, 127)
     for k in range(1, 4):
         remote(
@@ -355,9 +355,9 @@
             fixed_sem.at[0], fixed_sem.at[1],
             (lax.axis_index("dp"), torus.ys[k]),
         ).start()
-    send_rows(0, 16, 0)
-    pick(16, PHASES[1])
-    send_rows(16, PHASES[1], 0)
+    send_rows(0, 8, 0)
+    pick(8, PHASES[1])
+    send_rows(8, PHASES[1], 0)
     recv[0] = send[0]
 
     waiting = remote(

time: 70.1 us -> 68.9 us (0.983)
  Pallas kernels: 69.1 us -> 68 us
    pallas_call x1, Pallas kernels: 67.6 us -> 66.4 us  [step(): pl.pallas_call(step_kernel, out_shape=(jax.ShapeDtypeStruct((4, 256), F32...]
where the time goes in v6:
time: 68.9 us; the launch traced here: 68.8 us
  Pallas kernels  68 us (99%)
  between operations  0.82 us (1%)
    pallas_call x1, Pallas kernels, step(): pl.pallas_call(step_kernel, out_shape=(jax.ShapeDtypeStruct((4, 256), F32...  66.4 us
    pallas_call x1, Pallas kernels, hand_over(): pl.pallas_call(hand_over_kernel, out_shape=tuple((jax.ShapeDtypeStruct(x....  1.52 us

profile of v6, /device:TPU:1, one launch (start us, length us, event | category | flops | bytes accessed | tf_op | source)
XLA Modules:
  0.0 68.8 jit_solution(13473241200226621008)
XLA Ops:
  0.6 66.4 %step.1 = (f32[4,256]{1,0:T(4,128)}, f32[4]{0:T(128)}, f32[1,2048]{1,0:T(1,128)}) custom-call(bf16[16384,128]{1,0:T(8,128)(2,1)} %bitcast.6, s32[2,8192]{1,0:T(2,128)} %bitcast.7, f32[128,128]{1,0:T(8,128)} %w_hbm.1, s32[1,2048]{1,0:T(1,128)} %bitcast.8, s32[1,2048]{1,0:T(1,128)} %bitcast.9, bf16[2048,256]{1,0:T(8,128)(2,1)} %z_hbm.1, s32[1,512]{1,0:T(1,128)} %bitcast.10, ...), custom_call_target="tpu_custom_call" | custom-call | tf_op jit(solution)/shard_map/step/pallas_call | solution.py:482
  67.1 1.5 %hand_over.1 = (f32[4,256]{1,0:T(4,128)}, f32[4]{0:T(128)}, f32[1,2048]{1,0:T(1,128)}) custom-call(f32[4,256]{1,0:T(4,128)} %get-tuple-element.9.refs_0_, f32[4]{0:T(128)} %get-tuple-element.10.refs_1_, f32[1,2048]{1,0:T(1,128)} %get-tuple-element.11.refs_2_), custom_call_target="tpu_custom_call" | custom-call | tf_op jit(solution)/shard_map/hand_over/pallas_call | solution.py:537
